TPU v7x, 256 devices: a whole 4x4x8 slice. The times are simulated.
256 devices in a mesh: va: 8 (over x, y_lo), vb: 8 (over z), aux: 4 (over y_hi, core).
Axes of the slice: x: 4, y: 4 (y_hi: 2, y_lo: 2; y = y_hi * 2 + y_lo), z: 8, core: 2. Of those that a mesh axis runs over, the one named last changes fastest.
Arguments:
- factors: float32 [1024, 8, 2048], P(None, None, 'va'), may hold values from -0.046875 to 0.046875
- domains: int32 [8, 16, 8], replicated, may hold values from 0 to 1, as said below
- occ_energy: float32 [8], replicated, may hold values from -3 to -0.5
- vir_energy: float32 [2048], replicated, may hold values from 0.5 to 3
Outputs:
- amplitudes: float32 [8, 2048, 8, 2048], P(None, 'va', 'aux', 'vb')
Inputs may be any that keep to these rules, and one draw needn't show every extreme that they name: `domains`: for every occupied orbital and every block of 128 virtuals, exactly 6 of the 8 fitting blocks are 1.
All inputs are finite; a program needn't handle non-finite values.
Results may differ from a plain program's by a relative error of at most 0.000096.
Values sent between devices are 32-bit elements; how exact they have to be, the bound alone decides.
A program may use at most 128 MiB of HBM per device.

v0:
```python
import math

import jax
import jax.numpy as jnp
from jax import lax
from jax.sharding import PartitionSpec as P

O = 8
V = 2048
NAUX = 1024
BLK = 128


highest = lax.Precision.HIGHEST


def broadcast(block, axis, holder):
    block = jnp.where(lax.axis_index(axis) == holder, block, jnp.zeros_like(block))
    return lax.psum(block, axis)


def contract_first(left, right):
    return lax.dot_general(
        left, right, (((0,), (0,)), ((), ())), precision=highest, preferred_element_type=jnp.float32
    )


def spread_mask(domains):
    expanded = jnp.transpose(domains, (2, 0, 1)).astype(jnp.float32)
    fit_blocks, orbitals, vir_blocks = expanded.shape
    expanded = jnp.broadcast_to(
        expanded[:, None, :, :, None], (fit_blocks, BLK, orbitals, vir_blocks, BLK)
    )
    return expanded.reshape(fit_blocks * BLK, orbitals, vir_blocks * BLK)


def body(factors, domains, occ_energy, vir_energy):
    fit_rows = factors.shape[0]
    tile_width = factors.shape[2]
    block_count = tile_width // BLK
    local_occ = O // lax.axis_size("aux")
    va_index = lax.axis_index("va")
    vb_index = lax.axis_index("vb")
    aux_index = lax.axis_index("aux")
    mask_here = lax.dynamic_slice_in_dim(domains, va_index * block_count, block_count, 1)
    weights = spread_mask(mask_here)
    masked = factors * weights
    flattened = masked.reshape(fit_rows, O * tile_width)
    own_columns = lax.dynamic_slice_in_dim(masked, aux_index * local_occ, local_occ, 1)
    far_factors = broadcast(own_columns, "va", vb_index)
    far_factors = far_factors.reshape(fit_rows, local_occ * tile_width)
    vir_rows = lax.dynamic_slice_in_dim(vir_energy, va_index * tile_width, tile_width)
    vir_cols = lax.dynamic_slice_in_dim(vir_energy, vb_index * tile_width, tile_width)
    occ_columns = lax.dynamic_slice_in_dim(occ_energy, aux_index * local_occ, local_occ)
    denominator = (
        vir_rows[None, :, None, None]
        + vir_cols[None, None, None, :]
        - occ_energy[:, None, None, None]
        - occ_columns[None, None, :, None]
    )
    denominator = denominator.reshape(O * tile_width, local_occ * tile_width)
    direct = contract_first(flattened, far_factors)
    first_amps = -direct / denominator
    share = lax.psum_scatter(
        lax.dot_general(
            far_factors,
            first_amps,
            (((1,), (1,)), ((), ())),
            precision=highest,
            preferred_element_type=jnp.float32,
        ),
        ("vb", "aux"),
        scatter_dimension=0,
        tiled=True,
    )
    summed = lax.all_gather(share, ("vb", "aux"), axis=0, tiled=True)
    dressed = summed * weights.reshape(fit_rows, O * tile_width)
    dressed_own = lax.dynamic_slice_in_dim(
        dressed.reshape(fit_rows, O, tile_width), aux_index * local_occ, local_occ, 1
    )
    far_dressed = broadcast(dressed_own, "va", vb_index)
    far_dressed = far_dressed.reshape(fit_rows, local_occ * tile_width)
    residual = contract_first(flattened + 2.0 * dressed, far_factors + 2.0 * far_dressed)
    second_amps = -residual / denominator
    scaled = second_amps * (8.0 * O * V / math.sqrt(NAUX))
    return scaled.reshape(O, tile_width, local_occ, tile_width)


def solution(mesh):
    placed = (P(None, None, "va"), P(), P(), P())
    return jax.shard_map(
        body, mesh=mesh, in_specs=placed, out_specs=P(None, "va", "aux", "vb"), check_vma=False
    )
```

profile of v0, /device:TPU:14, one launch (start us, length us, event | category | flops | bytes accessed | tf_op | source)
XLA Modules:
  0.0 649.4 jit_solution(7066588114830620974)
XLA Ops:
  6.5 0.8 convert_bitcast_fusion
  7.4 5.5 broadcast_in_dim.2
  12.8 11.5 %reshape.66 = f32[1024,8,256]{2,1,0:T(8,128)} reshape(f32[8,128,8,2,128]{4,3,2,1,0:T(2,128)} %broadcast_in_dim.2) | data formatting | bytes 16777216 | tf_op jit(solution)/shard_map/reshape | solution.py:34
  24.4 8.7 %copy.11 = f32[1024,8,256]{0,2,1:T(8,128)} copy(f32[1024,8,256]{2,1,0:T(8,128)} %reshape.66) | data formatting | bytes 16777216 | tf_op jit(solution)/shard_map/reshape | solution.py:34
  33.1 8.8 %copy.8 = f32[1024,8,256]{0,2,1:T(8,128)} copy(f32[1024,8,256]{2,1,0:T(8,128)} %param.4) | data formatting | bytes 16777216 | tf_op args[0]
  41.8 12.0 %mul.42 = f32[1024,8,256]{0,2,1:T(8,128)} multiply(f32[1024,8,256]{0,2,1:T(8,128)} %copy.8, f32[1024,8,256]{0,2,1:T(8,128)} %copy.11) | non-fusion elementwise | flops 2097152 | bytes 25165824 | tf_op jit(solution)/shard_map/mul | solution.py:47
  53.8 3.2 dynamic-slice_select_fusion.1
  58.6 1.4 sub.41
  60.1 2.5 copy.14
  62.5 105.0 %all-reduce.3.cloned.1.call-done = f32[1024,512]{0,1:T(8,128)} async-done(((f32[1024,512]{0,1:T(8,128)}), f32[1024,512]{0,1:T(8,128)}) %all-reduce.3.cloned.1.call-update) | async-done | bytes 2097168 | tf_op jit(solution)/shard_map/psum | solution.py:19
  167.5 16.5 %fusion.13 = f32[2048,512]{1,0:T(8,128)S(1)} fusion(f32[1024,2048]{0,1:T(8,128)} %bitcast.17, f32[1024,512]{0,1:T(8,128)} %all-reduce.3.cloned.1.call-done), kind=kOutput, calls=%fused_computation.20 | convolution fusion | flops 12884901888 | bytes 14680064 | tf_op jit(solution)/shard_map/dot_general | solution.py:23
  184.0 29.1 %fusion.4 = f32[1024,2048]{1,0:T(8,128)} fusion(f32[1024,512]{0,1:T(8,128)S(1)} %copy-done.2, f32[2048,512]{1,0:T(8,128)S(1)} %fusion.13, f32[2048,512]{1,0:T(8,128)S(1)} %bitcast.23, f32[512]{0:T(512)S(1)} %bitcast.24), kind=kOutput, calls=%fused_computation.5 | convolution fusion | flops 12888047616 | bytes 18876416 | tf_op jit(solution)/shard_map/dot_general | solution.py:65
  213.2 156.5 %reduce-scatter.2.cloned.1.call-done = f32[32,2048]{1,0:T(8,128)} async-done(((f32[1024,2048]{1,0:T(8,128)}), f32[32,2048]{1,0:T(8,128)}) %reduce-scatter.2.cloned.1.call-update) | async-done | bytes 262160 | tf_op jit(solution)/shard_map/reduce_scatter | solution.py:64
  369.8 11.5 %reshape_reshape.3 = f32[1024,2048]{1,0:T(8,128)} reshape(f32[8,128,8,2,128]{4,3,2,1,0:T(2,128)} %broadcast_in_dim.2) | data formatting | bytes 16777216 | tf_op jit(solution)/shard_map/reshape;reshape | solution.py:77
  381.3 90.7 %all-gather.2.cloned.1.call-done = f32[1024,2048]{1,0:T(8,128)} async-done(((f32[32,2048]{1,0:T(8,128)}), f32[1024,2048]{1,0:T(8,128)}) %all-gather.2.cloned.1.call-update) | async-done | bytes 8388624 | tf_op jit(solution)/shard_map/all_gather | solution.py:76
  472.0 11.7 %mul.46 = f32[1024,2048]{1,0:T(8,128)} multiply(f32[1024,2048]{1,0:T(8,128)} %all-gather.2.cloned.1.call-done, f32[1024,2048]{1,0:T(8,128)} %reshape_reshape.3) | non-fusion elementwise | flops 2097152 | bytes 25165824 | tf_op jit(solution)/shard_map/mul | solution.py:77
  483.7 9.3 %copy.13 = f32[1024,2048]{0,1:T(8,128)} copy(f32[1024,2048]{1,0:T(8,128)} %mul.46) | data formatting | bytes 16777216 | tf_op jit(solution)/shard_map/reshape | solution.py:79
  493.0 3.2 dynamic-slice_select_fusion
  496.3 9.2 %copy.12 = f32[1024,2048]{1,0:T(8,128)} copy(f32[1024,2048]{0,1:T(8,128)} %bitcast.18) | data formatting | bytes 16777216 | tf_op jit(solution)/shard_map/reshape | solution.py:48
  505.5 96.3 %all-reduce.5.cloned.1.call-done = f32[1024,2,256]{0,2,1:T(8,128)} async-done(((f32[1024,2,256]{0,2,1:T(8,128)}), f32[1024,2,256]{0,2,1:T(8,128)}) %all-reduce.5.cloned.1.call-update) | async-done | bytes 2097168 | tf_op jit(solution)/shard_map/psum | solution.py:19
  601.8 1.9 broadcast_multiply_fusion
  604.2 1.6 copy-done
  605.8 31.0 %divide_multiply_fusion = f32[2048,512]{1,0:T(8,128)} fusion(f32[2048,512]{1,0:T(8,128)} %bitcast.22, f32[1024,512]{0,1:T(8,128)S(1)} %bitcast_add_fusion, f32[1024,2048]{1,0:T(8,128)S(1)} %copy-done, f32[1024,2048]{1,0:T(8,128)} %mul.46, f32[512]{0:T(512)S(1)} %bitcast.25), kind=kOutput, calls=%fused_computation.3 | convolution fusion | flops 12893290496 | bytes 27265024 | tf_op jit(solution)/shard_map/dot_general | solution.py:23
  636.8 5.9 reshape.65
  (23 shorter events, 2.1 us)
Async XLA Ops:
  6.5 161.0 %all-reduce.3.cloned.1.call-start = ((), (), s32[]{:S(2)}) async-start(), calls=%async_computation.1 | async-start | bytes 4194304 | tf_op jit(solution)/shard_map/psum | solution.py:19
  53.8 3.5 copy-start.3
  57.1 312.6 %reduce-scatter.2.cloned.1.call-start = ((), (), s32[]{:S(2)}) async-start(), calls=%async_computation.2 | async-start | bytes 8650752 | tf_op jit(solution)/shard_map/reduce_scatter | solution.py:64
  167.5 16.5 %copy-start.1 = (f32[256,8,2,256]{3,1,2,0:T(8,128)S(1)}, f32[256,8,2,256]{3,1,2,0:T(8,128)}, u32[]{:S(2)}) copy-start(f32[256,8,2,256]{3,1,2,0:T(8,128)} %copy.14) | copy-start | bytes 12582916
  167.5 16.5 %copy-start.2 = (f32[1024,512]{0,1:T(8,128)S(1)}, f32[1024,512]{0,1:T(8,128)}, u32[]{:S(2)}) copy-start(f32[1024,512]{0,1:T(8,128)} %all-reduce.3.cloned.1.call-done) | copy-start | bytes 6291460
  213.1 258.9 %all-gather.2.cloned.1.call-start = ((), (), s32[]{:S(2)}) async-start(), calls=%async_computation.3 | async-start | bytes 8650752 | tf_op jit(solution)/shard_map/all_gather | solution.py:76
  369.7 232.1 %all-reduce.5.cloned.1.call-start = ((), (), s32[]{:S(2)}) async-start(), calls=%async_computation.4 | async-start | bytes 4194304 | tf_op jit(solution)/shard_map/psum | solution.py:19
  601.8 4.0 copy-start
Sparse Core Ops, SparseCore 0:
  57.2 110.2 all-reduce.2
  213.3 156.3 reduce-scatter.1
  372.5 99.4 all-gather.1
  496.4 105.3 all-reduce.4
where the time goes:
time: 658 us; the launch traced here: 649 us
  waiting for transfers between devices  449 us (68%)
  local copies, waits for them, and re-layouts  76.8 us (12%)
  matrix products  76.6 us (12%)
  other arithmetic  33.7 us (5%)
  between operations  13.4 us (2%)
    psum x2, waiting for transfers between devices, broadcast(): return lax.psum(block, axis)  201 us
    reduce_scatter x1, waiting for transfers between devices, body(): lax.psum_scatter(lax.dot_general(far_factors, first_amps, (((1,), (1,)),...  157 us
    all_gather x1, waiting for transfers between devices, body(): summed = lax.all_gather(share, ('vb', 'aux'), axis=0, tiled=True)  90.7 us
    dot_general x2, matrix products, contract_first(): lax.dot_general(left, right, (((0,), (0,)), ((), ())), precision=highest,...  47.5 us
    dot_general x1, matrix products, body(): lax.dot_general(far_factors, first_amps, (((1,), (1,)), ((), ())), precis...  29.1 us
    reshape x2, local copies, waits for them, and re-layouts, spread_mask(): return expanded.reshape(fit_blocks * BLK, orbitals, vir_blocks * BLK)  20.2 us
  transfers between devices with their start and end apart: 4, of which 4 were waited for; matrix products, arithmetic and copies ran while one was open for 4% of the time, Pallas kernels for 0%

commit v1 on v0

v1 whole, which is shorter than its diff:
```python
import functools
import math

import jax
import jax.numpy as jnp
from jax import lax
from jax.experimental import pallas as pl
from jax.experimental.pallas import tpu as pltpu
from jax.sharding import PartitionSpec as P

O = 8
V = 2048
NAUX = 1024
BLK = 128
PRESENT = 6
NPB = 8
NVB = 16
TILE = 256
ROWS = O * TILE
PAIR = 2 * TILE
PACK = PRESENT * BLK
SLICE = PAIR // 8
HALF = SLICE // 2
CHUNKS = 8
LAG = 2
RING_LAG = 3
SCALE = 8.0 * O * V / math.sqrt(NAUX)
MESH = pl.DeviceIdType.MESH
F32 = jnp.float32
BF16 = jnp.bfloat16
VMEM_LIMIT = 60 * 1024 * 1024

TREES = (
    {0: (1,), 1: (2, 5), 2: (3, 6), 5: (4,), 6: (7,)},
    {0: (3,), 3: (2, 7), 2: (1,), 7: (4, 6), 6: (5,)},
    {0: (4,), 4: (5, 7), 5: (6, 1), 6: (2,), 7: (3,)},
)


def split(value):
    high = value.astype(BF16)
    return high, (value - high.astype(F32)).astype(BF16)


def dot_nt(left, right):
    return lax.dot_general(left, right, (((1,), (1,)), ((), ())), preferred_element_type=F32)


def dot_nn(left, right):
    return lax.dot_general(left, right, (((1,), (0,)), ((), ())), preferred_element_type=F32)


def unpack(table, slots, packed, block, high, low, row, scale=None):
    for p in range(NPB):
        entry = block * NPB + p
        slot = jnp.minimum(slots[entry], PRESENT - 1)
        keep = table[entry].astype(F32)
        value = packed(pl.ds(pl.multiple_of(slot * BLK, BLK), BLK)) * keep
        h, l = split(value)
        high[row : row + BLK, p * BLK : (p + 1) * BLK] = h
        low[row : row + BLK, p * BLK : (p + 1) * BLK] = l


def prep_kernel(table, slots, first, second, high, low, packed):
    p = pl.program_id(0)
    va = lax.axis_index("va")
    for i in range(O):
        for half, factors in enumerate((first, second)):
            entry = (i * NVB + va * 2 + half) * NPB + p
            keep = table[entry]
            block = factors[pl.ds(i, BLK, stride=O), :].T * keep.astype(F32)
            row = i * TILE + half * BLK
            h, l = split(block)
            high[row : row + BLK, :] = h
            low[row : row + BLK, :] = l
            slot = jnp.minimum(slots[entry], PRESENT - 1)

            @pl.when(keep > 0)
            def _():
                packed[row : row + BLK, pl.ds(pl.multiple_of(slot * BLK, BLK), BLK)] = block


def spread_kernel(packed, out, send, recv, local):
    va, vb, aux = lax.axis_index("va"), lax.axis_index("vb"), lax.axis_index("aux")
    barrier = pltpu.get_barrier_semaphore()
    for k in range(1, 8):
        pl.semaphore_signal(barrier, 1, device_id={"va": (va + k) % 8}, device_id_type=MESH)
    pl.semaphore_wait(barrier, 7)
    root_x, root_y = vb // 2, vb % 2
    node = (va // 2 - root_x + 4) % 4 + 4 * ((va % 2 + root_y) % 2)

    def lookup(values):
        found = jnp.int32(values[0])
        for n in range(1, 8):
            found = jnp.where(node == n, jnp.int32(values[n]), found)
        return found

    skews, childs = [], []
    for tree in TREES:
        depth = {0: 0}
        todo = [0]
        for n in todo:
            for member in tree.get(n, ()):
                depth[member] = depth[n] + 1
                todo.append(member)
        skews.append(lookup([LAG * depth[n] for n in range(8)]))
        childs.append([lookup([(*tree.get(n, ()), -1, -1)[k] for n in range(8)]) for k in range(2)])

    def copy(tree, chunk, child, member):
        ref = out.at[pl.ds(pl.multiple_of(chunk * SLICE, SLICE), SLICE), pl.ds(tree * 256, 256)]
        place = ((root_x + member % 4) % 4) * 2 + (root_y + member // 4) % 2
        return pltpu.make_async_remote_copy(
            ref, ref, send.at[tree, chunk, child], recv.at[tree, chunk], device_id={"va": place}, device_id_type=MESH
        )

    @pl.when(node == 0)
    def _():
        own = pltpu.make_async_copy(packed.at[pl.ds(pl.multiple_of(aux * PAIR, PAIR), PAIR), :], out, local)
        own.start()
        own.wait()

    def step(t, carry):
        for tree in range(3):
            chunk = t - skews[tree]

            @pl.when((chunk >= 0) & (chunk < CHUNKS))
            def _():
                @pl.when(node != 0)
                def _():
                    copy(tree, chunk, 0, 0).wait_recv()

                for k in range(2):
                    member = childs[tree][k]

                    @pl.when(member >= 0)
                    def _():
                        copy(tree, chunk, k, member).start()

        return carry

    lax.fori_loop(0, CHUNKS + 4 * LAG, step, 0)

    def drain(chunk, carry):
        for tree in range(3):
            for k in range(2):
                member = childs[tree][k]

                @pl.when(member >= 0)
                def _():
                    copy(tree, chunk, k, member).wait_send()

        return carry

    lax.fori_loop(0, CHUNKS, drain, 0)


def dress_kernel(table, slots, picks, cols, high, low, col_energy, row_energy, out, col_high, col_low, total):
    g = pl.program_id(0)
    vb, aux = lax.axis_index("vb"), lax.axis_index("aux")

    @pl.when(g == 0)
    def _():
        for q in range(4):
            block = (aux * 2 + q // 2) * NVB + vb * 2 + q % 2
            unpack(table, slots, lambda c: cols[q * BLK : (q + 1) * BLK, c], block, col_high, col_low, q * BLK)
        total[...] = jnp.zeros_like(total)

    ch, cl = col_high[...], col_low[...]
    parts_h, parts_l = [], []
    for i in range(2):
        rows = slice(i * TILE, (i + 1) * TILE)
        bh, bl = high[rows, :], low[rows, :]
        direct = dot_nt(ch, bh) + dot_nt(ch, bl) + dot_nt(cl, bh)
        energy = col_energy[...] + row_energy[0, i : i + 1, :]
        h, l = split(-direct / energy)
        parts_h.append(h)
        parts_l.append(l)
    th, tl = jnp.concatenate(parts_h, axis=1), jnp.concatenate(parts_l, axis=1)
    bh, bl = high[...], low[...]
    total[...] += dot_nn(th, bh) + dot_nn(th, bl) + dot_nn(tl, bh)

    @pl.when(g == 3)
    def _():
        for q in range(4):
            block = (aux * 2 + q // 2) * NVB + vb * 2 + q % 2
            rows = slice(q * BLK, (q + 1) * BLK)
            for k in range(PRESENT):
                pick = picks[block * NPB + k]
                out[rows, k * BLK : (k + 1) * BLK] = total[rows, pl.ds(pl.multiple_of(pick * BLK, BLK), BLK)]


def exchange_kernel(
    part, buf, relay, merged, recv,
    relay_s, relay_r, side_s, side_r, near_s, near_r, merge_s, merge_r,
    ag_s, ag_r, fwd_s, ex_s, ex_r, ring_s, ring_r, pair_s, pair_r,
):
    va, vb, aux = lax.axis_index("va"), lax.axis_index("vb"), lax.axis_index("aux")
    x, y = va // 2, va % 2
    core, hi = aux % 2, aux // 2
    right, left, across = (x + 1) % 4, (x + 3) % 4, (x + 2) % 4
    other = (aux + 2) % 4
    barrier = pltpu.get_barrier_semaphore()
    for k in range(1, 8):
        pl.semaphore_signal(barrier, 1, device_id={"va": (va + k) % 8}, device_id_type=MESH)
    pl.semaphore_signal(barrier, 1, device_id={"vb": (vb + 1) % 8}, device_id_type=MESH)
    pl.semaphore_signal(barrier, 1, device_id={"vb": (vb + 7) % 8}, device_id_type=MESH)
    partner = hi * 2 + (1 - core)
    pl.semaphore_signal(barrier, 1, device_id={"aux": partner}, device_id_type=MESH)

    @pl.when(va == vb)
    def _():
        for k in range(8):
            pl.semaphore_signal(barrier, 1, device_id={"va": (va + k) % 8, "aux": other}, device_id_type=MESH)

    pl.semaphore_wait(barrier, 11)

    def rows_of(owner, offset, size):
        return pl.ds(pl.multiple_of(owner * SLICE + offset, HALF), size)

    def put(src, dst, s, r, **device):
        return pltpu.make_async_remote_copy(src, dst, s, r, device_id=device, device_id_type=MESH)

    sends = []

    def go(copy):
        copy.start()
        sends.append(copy)

    for yy in range(2):
        far = across * 2 + yy
        go(put(part.at[rows_of(far, 0, HALF)], relay.at[0, yy], relay_s.at[0, yy], relay_r.at[0, yy], va=right * 2 + y))
        go(put(part.at[rows_of(far, HALF, HALF)], relay.at[1, yy], relay_s.at[1, yy], relay_r.at[1, yy], va=left * 2 + y))
    side = x * 2 + 1 - y
    go(put(part.at[rows_of(side, 0, SLICE)], recv.at[4], side_s, side_r, va=side))
    for yy in range(2):
        slot = (yy + y) % 2
        to_right, to_left = right * 2 + yy, left * 2 + yy
        go(put(part.at[rows_of(to_right, HALF, HALF)], recv.at[slot, pl.ds(HALF, HALF)], near_s.at[0, yy], near_r.at[slot], va=to_right))
        go(put(part.at[rows_of(to_left, 0, HALF)], recv.at[2 + slot, pl.ds(0, HALF)], near_s.at[1, yy], near_r.at[2 + slot], va=to_left))
    for yy in range(2):
        slot = (yy + y) % 2
        to_right, to_left = right * 2 + yy, left * 2 + yy
        put(relay.at[0, yy], relay.at[0, yy], relay_s.at[0, yy], relay_r.at[0, yy], va=va).wait_recv()
        merged[0, yy] = part[rows_of(to_right, 0, HALF)] + relay[0, yy]
        go(put(merged.at[0, yy], recv.at[slot, pl.ds(0, HALF)], merge_s.at[0, yy], merge_r.at[slot], va=to_right))
        put(relay.at[1, yy], relay.at[1, yy], relay_s.at[1, yy], relay_r.at[1, yy], va=va).wait_recv()
        merged[1, yy] = part[rows_of(to_left, HALF, HALF)] + relay[1, yy]
        go(put(merged.at[1, yy], recv.at[2 + slot, pl.ds(HALF, HALF)], merge_s.at[1, yy], merge_r.at[2 + slot], va=to_left))
    for slot in range(4):
        put(merged.at[0, 0], recv.at[slot, pl.ds(0, HALF)], near_s.at[0, 0], near_r.at[slot], va=va).wait_recv()
        put(merged.at[0, 0], recv.at[slot, pl.ds(0, HALF)], near_s.at[0, 0], merge_r.at[slot], va=va).wait_recv()
    put(recv.at[4], recv.at[4], side_s, side_r, va=va).wait_recv()

    mine = rows_of(va, 0, SLICE)

    def home(member):
        return jnp.where(member == vb, aux, 4)

    here = home(va)
    buf[here, mine] = part[mine] + ((recv[0] + recv[1]) + (recv[2] + recv[3])) + recv[4]

    own = buf.at[here, mine]
    targets = (right * 2 + y, left * 2 + y, x * 2 + 1 - y, right * 2 + 1 - y, left * 2 + 1 - y)
    for n, target in enumerate(targets):
        go(put(own, buf.at[home(target), mine], ag_s.at[n], ag_r.at[va, 0], va=target))
    go(put(own, buf.at[aux, mine], ex_s, ex_r.at[va], va=vb, aux=other))

    def arrived(owner, offset, size, part_index):
        ref = buf.at[here, rows_of(owner, offset, size)]
        put(ref, ref, ex_s, ag_r.at[owner, part_index], va=va).wait_recv()

    for n, yy in enumerate((y, 1 - y)):
        from_left, from_right = left * 2 + yy, right * 2 + yy
        arrived(from_left, 0, SLICE, 0)
        rows = rows_of(from_left, 0, HALF)
        go(put(buf.at[here, rows], buf.at[home(right * 2 + y), rows], fwd_s.at[0, n], ag_r.at[from_left, 0], va=right * 2 + y))
        arrived(from_right, 0, SLICE, 0)
        rows = rows_of(from_right, HALF, HALF)
        go(put(buf.at[here, rows], buf.at[home(left * 2 + y), rows], fwd_s.at[1, n], ag_r.at[from_right, 1], va=left * 2 + y))
    arrived(side, 0, SLICE, 0)
    for yy in range(2):
        arrived(across * 2 + yy, 0, HALF, 0)
        arrived(across * 2 + yy, HALF, HALF, 1)

    up, down = (vb + 1) % 8, (vb + 7) % 8
    distances = ((vb - va + 8) % 8, (va - vb + 8) % 8)
    owners = (va, side, *(m * 2 + yy for m in (right, left, across) for yy in (y, 1 - y)))

    def ring(step, way, what):
        h = step // 8
        owner = step % 8
        slice_owner = owners[7]
        for n in range(7):
            slice_owner = jnp.where(owner == n, owners[n], slice_owner)
        group = (hi + h) % 2
        ref = buf.at[group * 2 + core, rows_of(slice_owner, way * HALF, HALF)]
        if what == "ring":
            return put(ref, ref, ring_s.at[way, step], ring_r.at[way, step], vb=(up, down)[way])
        if what == "pair":
            return put(ref, ref, pair_s.at[way, step], pair_r.at[way, step], aux=partner)
        if what == "paired":
            other_ref = buf.at[group * 2 + 1 - core, rows_of(slice_owner, way * HALF, HALF)]
            return put(other_ref, other_ref, pair_s.at[way, step], pair_r.at[way, step], aux=partner)
        whole = buf.at[group * 2 + core, rows_of(slice_owner, 0, SLICE)]
        return put(whole, whole, ex_s, ex_r.at[slice_owner], vb=up)

    lags = [(RING_LAG * d) // 2 for d in distances]

    def ring_step(t, carry):
        for way in range(2):
            step = t - lags[way]

            @pl.when((step >= 0) & (step < 16))
            def _():
                @pl.when(va != vb)
                def _():
                    ring(step, way, "ring").wait_recv()

                if way == 0:

                    @pl.when((va == vb) & (step >= 8))
                    def _():
                        ring(step, way, "ex").wait_recv()

                @pl.when(distances[way] < 7)
                def _():
                    ring(step, way, "ring").start()

                ring(step, way, "pair").start()

        return carry

    lax.fori_loop(0, 16 + (RING_LAG * 7) // 2, ring_step, 0)

    def ring_drain(step, carry):
        for way in range(2):
            ring(step, way, "paired").wait_recv()
            ring(step, way, "pair").wait_send()

            @pl.when(distances[way] < 7)
            def _():
                ring(step, way, "ring").wait_send()

        return carry

    lax.fori_loop(0, 16, ring_drain, 0)

    for copy in sends:
        copy.wait_send()


def residual_kernel(where, table, slots, own, dressed, cols, col_dressed, row_energy, col_energy, out, row_high, row_low, col_high, col_low):
    g = pl.program_id(0)
    va, vb, aux = lax.axis_index("va"), lax.axis_index("vb"), lax.axis_index("aux")

    @pl.when(g == 0)
    def _():
        for q in range(4):
            block = (aux * 2 + q // 2) * NVB + vb * 2 + q % 2
            rows = slice(q * BLK, (q + 1) * BLK)
            unpack(table, slots, lambda c: cols[rows, c] + 2.0 * col_dressed[0, rows, c], block, col_high, col_low, q * BLK)

    for q in range(4):
        block = (g * 2 + q // 2) * NVB + va * 2 + q % 2
        rows = slice(q * BLK, (q + 1) * BLK)
        unpack(table, slots, lambda c: own[rows, c] + 2.0 * dressed[0, rows, c], block, row_high, row_low, q * BLK)
    ch, cl = col_high[...], col_low[...]
    for i in range(2):
        rows = slice(i * TILE, (i + 1) * TILE)
        rh, rl = row_high[rows, :], row_low[rows, :]
        total = dot_nt(rh, ch) + dot_nt(rh, cl) + dot_nt(rl, ch)
        result = -total / (row_energy[rows, :] + col_energy[...]) * SCALE
        out[i, :, 0, :] = result[:, :TILE]
        out[i, :, 1, :] = result[:, TILE:]


def body(factors, domains, occ_energy, vir_energy):
    va, vb, aux = lax.axis_index("va"), lax.axis_index("vb"), lax.axis_index("aux")
    blocks = jnp.arange(NPB, dtype=jnp.int32)
    slot_of = jnp.sum(jnp.where(blocks[:, None] > blocks[None, :], domains[:, :, None, :], 0), axis=-1)
    pick_of = jnp.sum(
        jnp.where((slot_of[:, :, None, :] == blocks[:, None]) & (domains[:, :, None, :] > 0), blocks, 0), axis=-1
    )
    table, slots, picks = domains.reshape(-1), slot_of.reshape(-1), pick_of.reshape(-1)
    vir_rows = lax.dynamic_slice_in_dim(vir_energy, va * TILE, TILE)
    vir_cols = lax.dynamic_slice_in_dim(vir_energy, vb * TILE, TILE)
    occ_cols = lax.dynamic_slice_in_dim(occ_energy, aux * 2, 2)
    row_energy = vir_rows[None, :] - occ_energy[:, None]
    col_energy = (vir_cols[None, :] - occ_cols[:, None]).reshape(PAIR)

    smem = pl.BlockSpec(memory_space=pltpu.SMEM)
    vmem = pl.BlockSpec(memory_space=pltpu.VMEM)
    whole = lambda shape: pl.BlockSpec(shape, lambda g: (0,) * len(shape))

    high, low, packed = pl.pallas_call(
        prep_kernel,
        grid=(NPB,),
        out_shape=(
            jax.ShapeDtypeStruct((ROWS, NAUX), BF16),
            jax.ShapeDtypeStruct((ROWS, NAUX), BF16),
            jax.ShapeDtypeStruct((ROWS, PACK), F32),
        ),
        in_specs=[smem, smem, pl.BlockSpec((BLK * O, BLK), lambda p: (p, 0)), pl.BlockSpec((BLK * O, BLK), lambda p: (p, 1))],
        out_specs=[
            pl.BlockSpec((ROWS, BLK), lambda p: (0, p)),
            pl.BlockSpec((ROWS, BLK), lambda p: (0, p)),
            whole((ROWS, PACK)),
        ],
        compiler_params=pltpu.CompilerParams(vmem_limit_bytes=VMEM_LIMIT),
        name="prep",
    )(table, slots, factors.reshape(NAUX * O, TILE), factors.reshape(NAUX * O, TILE))

    cols = pl.pallas_call(
        spread_kernel,
        out_shape=jax.ShapeDtypeStruct((PAIR, PACK), F32),
        in_specs=[pl.BlockSpec(memory_space=pl.ANY)],
        out_specs=vmem,
        scratch_shapes=[
            pltpu.SemaphoreType.DMA((3, CHUNKS, 2)),
            pltpu.SemaphoreType.DMA((3, CHUNKS)),
            pltpu.SemaphoreType.DMA,
        ],
        compiler_params=pltpu.CompilerParams(collective_id=0, has_side_effects=True, vmem_limit_bytes=VMEM_LIMIT),
        name="spread",
    )(packed)

    part = pl.pallas_call(
        dress_kernel,
        grid=(4,),
        out_shape=jax.ShapeDtypeStruct((PAIR, PACK), F32),
        in_specs=[
            smem, smem, smem,
            whole((PAIR, PACK)),
            pl.BlockSpec((PAIR, NAUX), lambda g: (g, 0)),
            pl.BlockSpec((PAIR, NAUX), lambda g: (g, 0)),
            whole((PAIR, 1)),
            pl.BlockSpec((1, 2, TILE), lambda g: (g, 0, 0)),
        ],
        out_specs=whole((PAIR, PACK)),
        scratch_shapes=[
            pltpu.VMEM((PAIR, NAUX), BF16),
            pltpu.VMEM((PAIR, NAUX), BF16),
            pltpu.VMEM((PAIR, NAUX), F32),
        ],
        compiler_params=pltpu.CompilerParams(vmem_limit_bytes=VMEM_LIMIT),
        name="dress",
    )(table, slots, picks, cols, high, low, col_energy.reshape(PAIR, 1), row_energy.reshape(4, 2, TILE))

    dma = pltpu.SemaphoreType.DMA
    buf = pl.pallas_call(
        exchange_kernel,
        out_shape=jax.ShapeDtypeStruct((5, PAIR, PACK), F32),
        in_specs=[vmem],
        out_specs=vmem,
        scratch_shapes=[
            pltpu.VMEM((2, 2, HALF, PACK), F32),
            pltpu.VMEM((2, 2, HALF, PACK), F32),
            pltpu.VMEM((5, SLICE, PACK), F32),
            dma((2, 2)), dma((2, 2)), dma, dma, dma((2, 2)), dma((4,)), dma((2, 2)), dma((4,)),
            dma((5,)), dma((8, 2)), dma((2, 2)), dma, dma((8,)), dma((2, 16)), dma((2, 16)), dma((2, 16)), dma((2, 16)),
        ],
        compiler_params=pltpu.CompilerParams(collective_id=1, has_side_effects=True, vmem_limit_bytes=VMEM_LIMIT),
        name="exchange",
    )(part)

    where = jnp.where(va == vb, aux, 4).astype(jnp.int32).reshape(1)
    return pl.pallas_call(
        residual_kernel,
        grid_spec=pltpu.PrefetchScalarGridSpec(
            num_scalar_prefetch=1,
            grid=(4,),
            in_specs=[
                smem, smem,
                pl.BlockSpec((PAIR, PACK), lambda g, w: (g, 0)),
                pl.BlockSpec((1, PAIR, PACK), lambda g, w: (g, 0, 0)),
                pl.BlockSpec((PAIR, PACK), lambda g, w: (0, 0)),
                pl.BlockSpec((1, PAIR, PACK), lambda g, w: (w[0], 0, 0)),
                pl.BlockSpec((PAIR, 1), lambda g, w: (g, 0)),
                pl.BlockSpec((1, PAIR), lambda g, w: (0, 0)),
            ],
            out_specs=pl.BlockSpec((2, TILE, 2, TILE), lambda g, w: (g, 0, 0, 0)),
            scratch_shapes=[pltpu.VMEM((PAIR, NAUX), BF16)] * 4,
        ),
        out_shape=jax.ShapeDtypeStruct((O, TILE, 2, TILE), F32),
        compiler_params=pltpu.CompilerParams(vmem_limit_bytes=VMEM_LIMIT),
        name="residual",
    )(where, table, slots, packed, buf, cols, buf, row_energy.reshape(ROWS, 1), col_energy.reshape(1, PAIR))


def solution(mesh):
    placed = (P(None, None, "va"), P(), P(), P())
    return jax.shard_map(
        body, mesh=mesh, in_specs=placed, out_specs=P(None, "va", "aux", "vb"), check_vma=False
    )
```

time: 658 us -> 221 us (0.34); the launches traced: 649 us -> 220 us
  waiting for transfers between devices: 449 us -> 0 us
  Pallas kernels: 0 us -> 210 us
  matrix products: 76.6 us -> 0 us
  local copies, waits for them, and re-layouts: 76.8 us -> 7.52 us
  other arithmetic: 33.7 us -> 3.26 us
  between operations: 13.4 us -> 0.05 us
    pallas_call x0 -> x5, Pallas kernels: none -> 210 us  [the longest x1 127 us: body(): pl.pallas_call(exchange_kernel, out_shape=jax.ShapeDtypeStruct((5, PAIR,...]
    psum x2 -> x0, waiting for transfers between devices: 201 us -> none  [broadcast(): return lax.psum(block, axis)]
    reduce_scatter x1 -> x0, waiting for transfers between devices: 157 us -> none  [body(): lax.psum_scatter(lax.dot_general(far_factors, first_amps, (((1,), (1,)),...]
    all_gather x1 -> x0, waiting for transfers between devices: 90.7 us -> none  [body(): summed = lax.all_gather(share, ('vb', 'aux'), axis=0, tiled=True)]
    dot_general x3 -> x0, matrix products: 76.6 us -> none  [the longest x2 47.5 us: contract_first(): lax.dot_general(left, right, (((0,), (0,)), ((), ())), precision=highest,...]
    reshape x5 -> x3, local copies, waits for them, and re-layouts: 44.6 us -> 2.07 us  [the longest x1 0.7 us: body(): slot_of.reshape(-1)]
    mul x3 -> x0, other arithmetic: 25.6 us -> none  [the longest x1 12 us: body(): masked = factors * weights]
    another operation x1 -> x0, local copies, waits for them, and re-layouts: 11.5 us -> none  [body(): dressed = summed * weights.reshape(fit_rows, O * tile_width)]
  transfers between devices with their start and end apart: 4 -> 0, of which waited for: 4 -> 0; matrix products, arithmetic and copies ran while one was open for 4% -> 0% of each run, Pallas kernels for 0% -> 0%
where the time goes in v1:
time: 221 us; the launch traced here: 220 us
  Pallas kernels  210 us (95%)
  local copies, waits for them, and re-layouts  7.52 us (3%)
  other arithmetic  3.26 us (1%)
    pallas_call x1, Pallas kernels, body(): pl.pallas_call(exchange_kernel, out_shape=jax.ShapeDtypeStruct((5, PAIR,...  127 us
    pallas_call x1, Pallas kernels, body(): pl.pallas_call(spread_kernel, out_shape=jax.ShapeDtypeStruct((PAIR, PACK)...  30.8 us
    pallas_call x1, Pallas kernels, body(): pl.pallas_call(dress_kernel, grid=(4,), out_shape=jax.ShapeDtypeStruct((P...  18.4 us
    pallas_call x1, Pallas kernels, body(): pl.pallas_call(prep_kernel, grid=(NPB,), out_shape=(jax.ShapeDtypeStruct(...  18.2 us
    pallas_call x1, Pallas kernels, body(): pl.pallas_call(residual_kernel, grid_spec=pltpu.PrefetchScalarGridSpec(nu...  14.6 us

profile of v1, /device:TPU:14, one launch (start us, length us, event | category | flops | bytes accessed | tf_op | source)
XLA Modules:
  0.0 220.4 jit_solution(12514422551022008445)
XLA Ops:
  0.0 0.7 dynamic_slice.10
  0.7 0.8 fusion.1
  1.5 0.1 subtract_bitcast_fusion.1
  1.6 0.0 copy-start
  1.6 0.7 sub.70
  2.3 0.7 broadcast_subtract_fusion.row_energy
  3.0 0.7 subtract_bitcast_fusion
  3.7 0.8 broadcast_compare_fusion
  4.5 0.9 select_reduce_fusion.1
  5.4 0.1 select_reduce_fusion
  5.5 0.1 copy.13
  5.6 0.7 reshape.104.slots
  6.3 0.1 copy.14
  6.4 0.7 reshape.106.picks
  7.1 0.8 copy.12
  7.9 0.7 reshape.103.table
  8.6 0.8 copy.18
  9.4 1.4 copy.20
  10.8 18.2 %prep.1 = (bf16[2048,1024]{1,0:T(8,128)(2,1)}, bf16[2048,1024]{1,0:T(8,128)(2,1)}, f32[2048,768]{1,0:T(8,128)}) custom-call(s32[1024]{0:T(1024)} %reshape.103.table, s32[1024]{0:T(1024)} %reshape.104.slots, f32[8192,256]{1,0:T(8,128)} %bitcast.15, f32[8192,256]{1,0:T(8,128)} %bitcast.16), custom_call_target="tpu_custom_call" | custom-call | tf_op jit(solution)/shard_map/prep/pallas_call | solution.py:395
  29.0 0.0 copy-done
  29.0 30.8 %spread.1.cols = f32[512,768]{1,0:T(8,128)} custom-call(f32[2048,768]{1,0:T(8,128)} %get-tuple-element.8.packed.own), custom_call_target="tpu_custom_call" | custom-call | tf_op jit(solution)/shard_map/spread/pallas_call | solution.py:413
  59.9 18.4 %dress.1.part = f32[512,768]{1,0:T(8,128)} custom-call(s32[1024]{0:T(1024)} %reshape.103.table, s32[1024]{0:T(1024)} %reshape.104.slots, s32[1024]{0:T(1024)} %reshape.106.picks, f32[512,768]{1,0:T(8,128)} %spread.1.cols, bf16[2048,1024]{1,0:T(8,128)(2,1)} %get-tuple-element.9.high, bf16[2048,1024]{1,0:T(8,128)(2,1)} %get-tuple-element.10.low, ...), custom_call_target="tpu_custom_call" | custom-call | tf_op jit(solution)/shard_map/dress/pallas_call | solution.py:427
  78.3 127.5 %exchange.1.dressed.col_dressed = f32[5,512,768]{2,1,0:T(8,128)} custom-call(f32[512,768]{1,0:T(8,128)} %dress.1.part), custom_call_target="tpu_custom_call" | custom-call | tf_op jit(solution)/shard_map/exchange/pallas_call | solution.py:450
  205.8 14.6 %residual.1 = f32[8,256,2,256]{3,2,1,0:T(2,128)} custom-call(s32[1]{0:T(128)} %bitcast.where, s32[1024]{0:T(1024)} %reshape.103.table, s32[1024]{0:T(1024)} %reshape.104.slots, f32[2048,768]{1,0:T(8,128)} %get-tuple-element.8.packed.own, f32[5,512,768]{2,1,0:T(8,128)} %exchange.1.dressed.col_dressed, f32[512,768]{1,0:T(8,128)} %spread.1.cols, ...), custom_call_target="tpu_custom_call" | custom-call | tf_op jit(solution)/shard_map/residual/pallas_call | solution.py:467
  (3 shorter events, 0.0 us)
Async XLA Ops:
  1.6 27.4 %copy-start = (f32[1,1,2,256]{3,1,2,0:T(1,128)}, f32[1,1,2,256]{3,1,2,0:T(1,128)S(1)}, u32[]{:S(2)}) copy-start(f32[1,1,2,256]{3,1,2,0:T(1,128)S(1)} %copy.17) | copy-start | bytes 6148

commit v2 on v0

v2 whole, which is shorter than its diff:
```python
import math

import jax
import jax.numpy as jnp
from jax import lax
from jax.experimental import pallas as pl
from jax.experimental.pallas import tpu as pltpu
from jax.sharding import PartitionSpec as P

O = 8
V = 2048
NAUX = 1024
BLK = 128
PRESENT = 6
NPB = 8
NVB = 16
TILE = 256
ROWS = O * TILE
PAIR = 2 * TILE
PACK = PRESENT * BLK
SLICE = PAIR // 8
HALF = SLICE // 2
CHUNKS = 8
STEPS = 16
LAG = 2
RING_LAG = 4
SCALE = 8.0 * O * V / math.sqrt(NAUX)
MESH = pl.DeviceIdType.MESH
F32 = jnp.float32
BF16 = jnp.bfloat16
VMEM_LIMIT = 60 * 1024 * 1024

TREES = (
    {0: (1,), 1: (2, 5), 2: (3, 6), 5: (4,), 6: (7,)},
    {0: (3,), 3: (2, 7), 2: (1,), 7: (4, 6), 6: (5,)},
    {0: (4,), 4: (5, 7), 5: (6, 1), 6: (2,), 7: (3,)},
)


def split(value):
    high = value.astype(BF16)
    return high, (value - high.astype(F32)).astype(BF16)


def dot_nt(left, right):
    return lax.dot_general(left, right, (((1,), (1,)), ((), ())), preferred_element_type=F32)


def dot_nn(left, right):
    return lax.dot_general(left, right, (((1,), (0,)), ((), ())), preferred_element_type=F32)


def kernel(
    domains, occ, vir, factors, out,
    raw, high, low, cols, col_high, col_low, total, part, buf, relay, merged, recv, row_high, row_low,
    row_weights, col_weights,
    load, spread_s, spread_r,
    relay_s, relay_r, side_s, side_r, near_s, near_r, merge_s, merge_r,
    ag_s, ag_r, fwd_s, ring_s, ring_r, pair_s, pair_r, far_s, far_r, last_s, last_r,
):
    va, vb, aux = lax.axis_index("va"), lax.axis_index("vb"), lax.axis_index("aux")
    x, y = va // 2, va % 2
    core, hi = aux % 2, aux // 2
    right, left, across = (x + 1) % 4, (x + 3) % 4, (x + 2) % 4
    partner, far, corner = hi * 2 + (1 - core), (aux + 2) % 4, ((1 - hi) * 2) + (1 - core)

    barrier = pltpu.get_barrier_semaphore()
    for k in range(1, 8):
        pl.semaphore_signal(barrier, 1, device_id={"va": (va + k) % 8}, device_id_type=MESH)
    pl.semaphore_signal(barrier, 1, device_id={"vb": (vb + 1) % 8}, device_id_type=MESH)
    pl.semaphore_signal(barrier, 1, device_id={"vb": (vb + 7) % 8}, device_id_type=MESH)
    pl.semaphore_signal(barrier, 1, device_id={"aux": partner}, device_id_type=MESH)
    pl.semaphore_signal(barrier, 1, device_id={"aux": far}, device_id_type=MESH)

    def fetch(p, half):
        rows = pl.ds(p * BLK * O, BLK * O)
        return pltpu.make_async_copy(factors.at[rows, pl.ds(half * BLK, BLK)], raw.at[half, rows], load.at[p, half])

    for p in range(NPB):
        for half in range(2):
            fetch(p, half).start()

    def weigh(table, n, i, block):
        absent = jnp.float32(0)
        for p in range(NPB):
            keep = domains[i, block, p].astype(F32)
            table[(n * NPB + p) * 3] = keep * (1.0 - absent) * (2.0 - absent) * 0.5
            table[(n * NPB + p) * 3 + 1] = keep * absent * (2.0 - absent)
            table[(n * NPB + p) * 3 + 2] = keep * absent * (absent - 1.0) * 0.5
            absent += 1.0 - keep

    def row_tables(n, carry):
        weigh(row_weights, n, n // 2, va * 2 + n % 2)
        return carry

    def col_tables(n, carry):
        weigh(col_weights, n, aux * 2 + n // 2, vb * 2 + n % 2)
        return carry

    lax.fori_loop(0, O * 2, row_tables, 0)
    lax.fori_loop(0, 4, col_tables, 0)

    def slot_of(n, k, full):
        values = [col_weights[(n * NPB + k + d) * 3 + d] * full(k + d) for d in range(3)]
        return values[0] + values[1] + values[2]

    def block_of(table, n, p, slots):
        values = [table[(n * NPB + p) * 3 + d] * slots(p - d) for d in range(3) if 0 <= p - d < PRESENT]
        return sum(values[1:], values[0])

    def lanes(slot):
        return pl.ds(pl.multiple_of(slot * BLK, BLK), BLK)

    def turned(i, half, p):
        keep = domains[i, va * 2 + half, p].astype(F32)
        return raw[half, pl.ds(p * (BLK * O) + i, BLK, stride=O), :].T * keep

    root_x, root_y = vb // 2, vb % 2
    node = (x - root_x + 4) % 4 + 4 * ((y + root_y) % 2)

    for p in range(NPB):
        for half in range(2):
            fetch(p, half).wait()

    @pl.when(node == 0)
    def _():
        def own(n, carry):
            i, half = aux * 2 + n // 2, n % 2
            rows = pl.ds(pl.multiple_of(n * BLK, BLK), BLK)
            for p in range(NPB):
                total[rows, p * BLK : (p + 1) * BLK] = turned(i, half, p)
            for k in range(PRESENT):
                cols[rows, k * BLK : (k + 1) * BLK] = slot_of(n, k, lambda p: total[rows, p * BLK : (p + 1) * BLK])
            return carry

        lax.fori_loop(0, 4, own, 0)

    def lookup(values):
        found = jnp.int32(values[0])
        for n in range(1, 8):
            found = jnp.where(node == n, jnp.int32(values[n]), found)
        return found

    skews, childs = [], []
    for tree in TREES:
        depth = {0: 0}
        todo = [0]
        for n in todo:
            for member in tree.get(n, ()):
                depth[member] = depth[n] + 1
                todo.append(member)
        skews.append(lookup([LAG * depth[n] for n in range(8)]))
        childs.append([lookup([(*tree.get(n, ()), -1, -1)[k] for n in range(8)]) for k in range(2)])

    def spread(tree, chunk, child, member):
        ref = cols.at[pl.ds(pl.multiple_of(chunk * SLICE, SLICE), SLICE), pl.ds(tree * 256, 256)]
        place = ((root_x + member % 4) % 4) * 2 + (root_y + member // 4) % 2
        return pltpu.make_async_remote_copy(
            ref, ref, spread_s.at[tree, chunk, child], spread_r.at[tree, chunk], device_id={"va": place}, device_id_type=MESH
        )

    pl.semaphore_wait(barrier, 11)

    def step(t, carry):
        for tree in range(3):
            chunk = t - skews[tree]

            @pl.when((chunk >= 0) & (chunk < CHUNKS))
            def _():
                @pl.when(node != 0)
                def _():
                    spread(tree, chunk, 0, 0).wait_recv()

                for k in range(2):
                    member = childs[tree][k]

                    @pl.when(member >= 0)
                    def _():
                        spread(tree, chunk, k, member).start()

        p = t // 2
        for n in range(4):
            i = (t % 2) * 4 + n
            for half in range(2):
                h, l = split(turned(i, half, p))
                rows = pl.ds(pl.multiple_of(i * TILE + half * BLK, BLK), BLK)
                high[rows, lanes(p)] = h
                low[rows, lanes(p)] = l
        return carry

    lax.fori_loop(0, STEPS, step, 0)

    def spread_drain(chunk, carry):
        for tree in range(3):
            for k in range(2):
                member = childs[tree][k]

                @pl.when(member >= 0)
                def _():
                    spread(tree, chunk, k, member).wait_send()

        return carry

    def energy_row(tile):
        return [vir[pl.ds(tile * 2 + half, 1), :] for half in range(2)]

    def energy_column(rows):
        return jnp.concatenate([jnp.broadcast_to(row, (8, BLK)).T[:, :1] for row in rows], axis=0)

    rows_a, rows_b = energy_row(va), energy_row(vb)
    row_a = jnp.concatenate(rows_a, axis=1)
    occ_j = [occ[aux * 2 + j] for j in range(2)]
    row_b = jnp.concatenate([row - occ_j[j] for j in range(2) for row in rows_b], axis=1)
    column_a = energy_column(rows_a)
    column_b = energy_column([row - occ_j[j] for j in range(2) for row in rows_b])

    def col_unpack(n, extra):
        rows = pl.ds(pl.multiple_of(n * BLK, BLK), BLK)
        for p in range(NPB):
            h, l = split(block_of(col_weights, n, p, lambda s: extra(rows, slice(s * BLK, (s + 1) * BLK))))
            col_high[rows, p * BLK : (p + 1) * BLK] = h
            col_low[rows, p * BLK : (p + 1) * BLK] = l

    def first_cols(n, carry):
        col_unpack(n, lambda rows, there: cols[rows, there])
        return carry

    lax.fori_loop(0, 4, first_cols, 0)
    total[...] = jnp.zeros_like(total)

    def dress(g, carry):
        ch, cl = col_high[...], col_low[...]
        parts_h, parts_l = [], []
        for i in range(2):
            rows = pl.ds(pl.multiple_of(g * PAIR + i * TILE, TILE), TILE)
            bh, bl = high[rows, :], low[rows, :]
            direct = dot_nt(ch, bh) + dot_nt(ch, bl) + dot_nt(cl, bh)
            energy = column_b + (row_a - occ[g * 2 + i])
            h, l = split(-direct / energy)
            parts_h.append(h)
            parts_l.append(l)
        th, tl = jnp.concatenate(parts_h, axis=1), jnp.concatenate(parts_l, axis=1)
        rows = pl.ds(pl.multiple_of(g * PAIR, PAIR), PAIR)
        bh, bl = high[rows, :], low[rows, :]
        total[...] += dot_nn(th, bh) + dot_nn(th, bl) + dot_nn(tl, bh)
        return carry

    lax.fori_loop(0, 4, dress, 0)

    def pack(n, carry):
        rows = pl.ds(pl.multiple_of(n * BLK, BLK), BLK)
        for k in range(PRESENT):
            part[rows, k * BLK : (k + 1) * BLK] = slot_of(n, k, lambda p: total[rows, p * BLK : (p + 1) * BLK])
        return carry

    lax.fori_loop(0, 4, pack, 0)

    def rows_of(owner, offset, size):
        return pl.ds(pl.multiple_of(owner * SLICE + offset, HALF), size)

    def put(src, dst, s, r, **device):
        return pltpu.make_async_remote_copy(src, dst, s, r, device_id=device, device_id_type=MESH)

    sends = []

    def go(copy):
        copy.start()
        sends.append(copy)

    for yy in range(2):
        opposite = across * 2 + yy
        go(put(part.at[rows_of(opposite, 0, HALF)], relay.at[0, yy], relay_s.at[0, yy], relay_r.at[0, yy], va=right * 2 + y))
        go(put(part.at[rows_of(opposite, HALF, HALF)], relay.at[1, yy], relay_s.at[1, yy], relay_r.at[1, yy], va=left * 2 + y))
    side = x * 2 + 1 - y
    go(put(part.at[rows_of(side, 0, SLICE)], recv.at[4], side_s, side_r, va=side))
    for yy in range(2):
        slot = (yy + y) % 2
        to_right, to_left = right * 2 + yy, left * 2 + yy
        go(put(part.at[rows_of(to_right, HALF, HALF)], recv.at[slot, pl.ds(HALF, HALF)], near_s.at[0, yy], near_r.at[slot], va=to_right))
        go(put(part.at[rows_of(to_left, 0, HALF)], recv.at[2 + slot, pl.ds(0, HALF)], near_s.at[1, yy], near_r.at[2 + slot], va=to_left))
    for yy in range(2):
        slot = (yy + y) % 2
        to_right, to_left = right * 2 + yy, left * 2 + yy
        put(relay.at[0, yy], relay.at[0, yy], relay_s.at[0, yy], relay_r.at[0, yy], va=va).wait_recv()
        merged[0, yy] = part[rows_of(to_right, 0, HALF)] + relay[0, yy]
        go(put(merged.at[0, yy], recv.at[slot, pl.ds(0, HALF)], merge_s.at[0, yy], merge_r.at[slot], va=to_right))
        put(relay.at[1, yy], relay.at[1, yy], relay_s.at[1, yy], relay_r.at[1, yy], va=va).wait_recv()
        merged[1, yy] = part[rows_of(to_left, HALF, HALF)] + relay[1, yy]
        go(put(merged.at[1, yy], recv.at[2 + slot, pl.ds(HALF, HALF)], merge_s.at[1, yy], merge_r.at[2 + slot], va=to_left))
    for slot in range(4):
        put(merged.at[0, 0], recv.at[slot, pl.ds(0, HALF)], near_s.at[0, 0], near_r.at[slot], va=va).wait_recv()
        put(merged.at[0, 0], recv.at[slot, pl.ds(0, HALF)], near_s.at[0, 0], merge_r.at[slot], va=va).wait_recv()
    put(recv.at[4], recv.at[4], side_s, side_r, va=va).wait_recv()

    mine = rows_of(va, 0, SLICE)

    def home(member):
        return jnp.where(member == vb, aux, 4)

    here = home(va)
    buf[here, mine] = part[mine] + ((recv[0] + recv[1]) + (recv[2] + recv[3])) + recv[4]

    own = buf.at[here, mine]
    targets = (right * 2 + y, left * 2 + y, x * 2 + 1 - y, right * 2 + 1 - y, left * 2 + 1 - y)
    for n, target in enumerate(targets):
        go(put(own, buf.at[home(target), mine], ag_s.at[n], ag_r.at[va, 0], va=target))

    def arrived(owner, offset, size, part_index):
        ref = buf.at[here, rows_of(owner, offset, size)]
        put(ref, ref, side_s, ag_r.at[owner, part_index], va=va).wait_recv()

    for n, yy in enumerate((y, 1 - y)):
        from_left, from_right = left * 2 + yy, right * 2 + yy
        arrived(from_left, 0, SLICE, 0)
        rows = rows_of(from_left, 0, HALF)
        go(put(buf.at[here, rows], buf.at[home(right * 2 + y), rows], fwd_s.at[0, n], ag_r.at[from_left, 0], va=right * 2 + y))
        arrived(from_right, 0, SLICE, 0)
        rows = rows_of(from_right, HALF, HALF)
        go(put(buf.at[here, rows], buf.at[home(left * 2 + y), rows], fwd_s.at[1, n], ag_r.at[from_right, 1], va=left * 2 + y))
    arrived(side, 0, SLICE, 0)
    for yy in range(2):
        arrived(across * 2 + yy, 0, HALF, 0)
        arrived(across * 2 + yy, HALF, HALF, 1)

    up, down = (vb + 1) % 8, (vb + 7) % 8
    distances = ((vb - va + 8) % 8, (va - vb + 8) % 8)
    owners = (va, side, *(m * 2 + yy for m in (right, left, across) for yy in (y, 1 - y)))

    def chunk_rows(step, way):
        owner = owners[7]
        for n in range(7):
            owner = jnp.where(step == n, owners[n], owner)
        return rows_of(owner, way * HALF, HALF)

    def ring(group, step, way, sems, **device):
        ref = buf.at[group, chunk_rows(step, way)]
        return put(ref, ref, sems[0].at[way, step], sems[1].at[way, step], **device)

    ring_sems, pair_sems, far_sems, last_sems = (ring_s, ring_r), (pair_s, pair_r), (far_s, far_r), (last_s, last_r)
    lags = [(RING_LAG * d) // 2 for d in distances]

    def ring_step(t, carry):
        for way in range(2):
            step = t - lags[way]
            toward = (up, down)[way]

            @pl.when((step >= 0) & (step < 8))
            def _():
                @pl.when(va != vb)
                def _():
                    ring(aux, step, way, ring_sems, va=va).wait_recv()

                @pl.when(distances[way] < 7)
                def _():
                    ring(aux, step, way, ring_sems, vb=toward).start()

                ring(aux, step, way, far_sems, aux=far).start()
                ring(aux, step, way, pair_sems, aux=partner).start()

        return carry

    lax.fori_loop(0, 8 + (RING_LAG * 7) // 2, ring_step, 0)

    def second_cols(n, carry):
        col_unpack(n, lambda rows, there: cols[rows, there] + 2.0 * buf[here, rows, there])
        return carry

    lax.fori_loop(0, 4, second_cols, 0)

    def residual(group):
        for i in range(2):
            orbital = group * 2 + i
            for half in range(2):
                rows = pl.ds(pl.multiple_of(orbital * TILE + half * BLK, BLK), BLK)
                here_rows = pl.ds(i * TILE + half * BLK, BLK)
                for p in range(NPB):
                    block = slice(p * BLK, (p + 1) * BLK)
                    value = high[rows, block].astype(F32) + low[rows, block].astype(F32)
                    change = block_of(
                        row_weights, orbital * 2 + half, p, lambda s: buf[group, here_rows, s * BLK : (s + 1) * BLK]
                    )
                    h, l = split(value + 2.0 * change)
                    row_high[half * BLK : (half + 1) * BLK, block] = h
                    row_low[half * BLK : (half + 1) * BLK, block] = l
            rh, rl = row_high[...], row_low[...]
            ch, cl = col_high[...], col_low[...]
            result = dot_nt(rh, ch) + dot_nt(rh, cl) + dot_nt(rl, ch)
            result = -result / ((column_a - occ[orbital]) + row_b) * SCALE
            out[orbital, :, 0, :] = result[:, :TILE]
            out[orbital, :, 1, :] = result[:, TILE:]

    def wait_chunks(group, sems):
        def one(step, carry):
            for way in range(2):
                ring(group, step, way, sems, va=va).wait_recv()
            return carry

        lax.fori_loop(0, 8, one, 0)

    def phase(n, carry):
        group = jnp.where(n == 0, aux, jnp.where(n == 1, partner, jnp.where(n == 2, far, corner)))

        @pl.when(n == 1)
        def _():
            wait_chunks(partner, pair_sems)

        @pl.when(n == 2)
        def _():
            def onward(step, carry):
                for way in range(2):
                    ring(far, step, way, far_sems, va=va).wait_recv()
                    ring(far, step, way, last_sems, aux=partner).start()
                return carry

            lax.fori_loop(0, 8, onward, 0)

        @pl.when(n == 3)
        def _():
            wait_chunks(corner, last_sems)

        residual(group)
        return carry

    lax.fori_loop(0, 4, phase, 0)

    def ring_drain(step, carry):
        for way in range(2):
            ring(aux, step, way, pair_sems, aux=partner).wait_send()
            ring(aux, step, way, far_sems, aux=far).wait_send()
            ring(far, step, way, last_sems, aux=partner).wait_send()

            @pl.when(distances[way] < 7)
            def _():
                ring(aux, step, way, ring_sems, vb=up).wait_send()

        return carry

    lax.fori_loop(0, 8, ring_drain, 0)
    lax.fori_loop(0, CHUNKS, spread_drain, 0)
    for copy in sends:
        copy.wait_send()


def body(factors, domains, occ_energy, vir_energy):
    smem = pl.BlockSpec(memory_space=pltpu.SMEM)
    vmem = pl.BlockSpec(memory_space=pltpu.VMEM)
    dma = pltpu.SemaphoreType.DMA
    return pl.pallas_call(
        kernel,
        out_shape=jax.ShapeDtypeStruct((O, TILE, 2, TILE), F32),
        in_specs=[smem, smem, vmem, pl.BlockSpec(memory_space=pl.ANY)],
        out_specs=vmem,
        scratch_shapes=[
            pltpu.VMEM((2, NAUX * O, BLK), F32),
            pltpu.VMEM((ROWS, NAUX), BF16),
            pltpu.VMEM((ROWS, NAUX), BF16),
            pltpu.VMEM((PAIR, PACK), F32),
            pltpu.VMEM((PAIR, NAUX), BF16),
            pltpu.VMEM((PAIR, NAUX), BF16),
            pltpu.VMEM((PAIR, NAUX), F32),
            pltpu.VMEM((PAIR, PACK), F32),
            pltpu.VMEM((5, PAIR, PACK), F32),
            pltpu.VMEM((2, 2, HALF, PACK), F32),
            pltpu.VMEM((2, 2, HALF, PACK), F32),
            pltpu.VMEM((5, SLICE, PACK), F32),
            pltpu.VMEM((TILE, NAUX), BF16),
            pltpu.VMEM((TILE, NAUX), BF16),
            pltpu.SMEM((O * 2 * NPB * 3,), F32),
            pltpu.SMEM((4 * NPB * 3,), F32),
            dma((NPB, 2)), dma((3, CHUNKS, 2)), dma((3, CHUNKS)),
            dma((2, 2)), dma((2, 2)), dma, dma, dma((2, 2)), dma((4,)), dma((2, 2)), dma((4,)),
            dma((5,)), dma((8, 2)), dma((2, 2)),
            dma((2, 8)), dma((2, 8)), dma((2, 8)), dma((2, 8)), dma((2, 8)), dma((2, 8)), dma((2, 8)), dma((2, 8)),
        ],
        compiler_params=pltpu.CompilerParams(collective_id=0, has_side_effects=True, vmem_limit_bytes=VMEM_LIMIT),
        name="amplitudes",
    )(domains, occ_energy, vir_energy.reshape(NVB, BLK), factors.reshape(NAUX * O, TILE))


def solution(mesh):
    placed = (P(None, None, "va"), P(), P(), P())
    return jax.shard_map(
        body, mesh=mesh, in_specs=placed, out_specs=P(None, "va", "aux", "vb"), check_vma=False
    )
```

time: 658 us -> 143 us (0.22); the launches traced: 649 us -> 142 us
  waiting for transfers between devices: 449 us -> 0 us
  Pallas kernels: 0 us -> 135 us
  matrix products: 76.6 us -> 0 us
  local copies, waits for them, and re-layouts: 76.8 us -> 7.11 us
  other arithmetic: 33.7 us -> 0 us
  between operations: 13.4 us -> 0.01 us
    psum x2 -> x0, waiting for transfers between devices: 201 us -> none  [broadcast(): return lax.psum(block, axis)]
    reduce_scatter x1 -> x0, waiting for transfers between devices: 157 us -> none  [body(): lax.psum_scatter(lax.dot_general(far_factors, first_amps, (((1,), (1,)),...]
    pallas_call x0 -> x1, Pallas kernels: none -> 135 us  [body(): pl.pallas_call(kernel, out_shape=jax.ShapeDtypeStruct((O, TILE, 2, TILE),...]
    all_gather x1 -> x0, waiting for transfers between devices: 90.7 us -> none  [body(): summed = lax.all_gather(share, ('vb', 'aux'), axis=0, tiled=True)]
    dot_general x3 -> x0, matrix products: 76.6 us -> none  [the longest x2 47.5 us: contract_first(): lax.dot_general(left, right, (((0,), (0,)), ((), ())), precision=highest,...]
    reshape x5 -> x0, local copies, waits for them, and re-layouts: 44.6 us -> none  [the longest x2 20.2 us: spread_mask(): return expanded.reshape(fit_blocks * BLK, orbitals, vir_blocks * BLK)]
    mul x3 -> x0, other arithmetic: 25.6 us -> none  [the longest x1 12 us: body(): masked = factors * weights]
    another operation x1 -> x0, local copies, waits for them, and re-layouts: 11.5 us -> none  [body(): dressed = summed * weights.reshape(fit_rows, O * tile_width)]
  transfers between devices with their start and end apart: 4 -> 0, of which waited for: 4 -> 0; matrix products, arithmetic and copies ran while one was open for 4% -> 0% of each run, Pallas kernels for 0% -> 0%
where the time goes in v2:
time: 143 us; the launch traced here: 142 us
  Pallas kernels  135 us (94%)
  local copies, waits for them, and re-layouts  7.11 us (5%)
    pallas_call x1, Pallas kernels, body(): pl.pallas_call(kernel, out_shape=jax.ShapeDtypeStruct((O, TILE, 2, TILE),...  135 us
    unnamed x2, local copies, waits for them, and re-layouts  7.11 us

profile of v2, /device:TPU:14, one launch (start us, length us, event | category | flops | bytes accessed | tf_op | source)
XLA Modules:
  0.0 142.4 jit_solution(13790732861453965060)
XLA Ops:
  0.0 1.5 %copy.5.domains = s32[8,16,8]{2,1,0:T(8,128)} copy(s32[8,16,8]{1,2,0:T(8,128)} %param.5) | data formatting | bytes 8192 | tf_op args[1]
  1.5 135.3 %amplitudes.1 = f32[8,256,2,256]{3,2,1,0:T(2,128)} custom-call(s32[8,16,8]{2,1,0:T(8,128)} %copy.5.domains, f32[8]{0:T(128)} %occ.1, f32[16,128]{1,0:T(8,128)} %bitcast.3, f32[8192,256]{1,0:T(8,128)} %bitcast.2), custom_call_target="tpu_custom_call" | custom-call | tf_op jit(solution)/shard_map/amplitudes/pallas_call | solution.py:448
  136.8 5.6 %copy.7 = f32[8,256,2,256]{3,2,1,0:T(2,128)} copy(f32[8,256,2,256]{3,2,1,0:T(2,128)} %amplitudes.1) | data formatting | bytes 8388608

commit v3 on v2

--- a/solution.py
+++ b/solution.py
@@ -22,6 +22,8 @@
 HALF = SLICE // 2
 CHUNKS = 8
 STEPS = 16
+LEAD = 5
+EARLY = 3
 LAG = 2
 RING_LAG = 4
 SCALE = 8.0 * O * V / math.sqrt(NAUX)
@@ -83,7 +85,7 @@
     def weigh(table, n, i, block):
         absent = jnp.float32(0)
         for p in range(NPB):
-            keep = domains[i, block, p].astype(F32)
+            keep = domains[i, p, block].astype(F32)
             table[(n * NPB + p) * 3] = keep * (1.0 - absent) * (2.0 - absent) * 0.5
             table[(n * NPB + p) * 3 + 1] = keep * absent * (2.0 - absent)
             table[(n * NPB + p) * 3 + 2] = keep * absent * (absent - 1.0) * 0.5
@@ -112,7 +114,7 @@
         return pl.ds(pl.multiple_of(slot * BLK, BLK), BLK)
 
     def turned(i, half, p):
-        keep = domains[i, va * 2 + half, p].astype(F32)
+        keep = domains[i, p, va * 2 + half].astype(F32)
         return raw[half, pl.ds(p * (BLK * O) + i, BLK, stride=O), :].T * keep
 
     root_x, root_y = vb // 2, vb % 2
@@ -149,7 +151,7 @@
             for member in tree.get(n, ()):
                 depth[member] = depth[n] + 1
                 todo.append(member)
-        skews.append(lookup([LAG * depth[n] for n in range(8)]))
+        skews.append(lookup([LEAD + LAG * (depth[n] - 1) for n in range(8)]))
         childs.append([lookup([(*tree.get(n, ()), -1, -1)[k] for n in range(8)]) for k in range(2)])
 
     def spread(tree, chunk, child, member):
@@ -161,16 +163,22 @@
 
     pl.semaphore_wait(barrier, 11)
 
+    @pl.when(node == 0)
+    def _():
+        def launch(chunk, carry):
+            for tree in range(3):
+                spread(tree, chunk, 0, childs[tree][0]).start()
+            return carry
+
+        lax.fori_loop(0, CHUNKS, launch, 0)
+
     def step(t, carry):
         for tree in range(3):
             chunk = t - skews[tree]
 
-            @pl.when((chunk >= 0) & (chunk < CHUNKS))
+            @pl.when((node != 0) & (chunk >= 0) & (chunk < CHUNKS))
             def _():
-                @pl.when(node != 0)
-                def _():
-                    spread(tree, chunk, 0, 0).wait_recv()
-
+                spread(tree, chunk, 0, 0).wait_recv()
                 for k in range(2):
                     member = childs[tree][k]
 
@@ -178,17 +186,20 @@
                     def _():
                         spread(tree, chunk, k, member).start()
 
-        p = t // 2
-        for n in range(4):
-            i = (t % 2) * 4 + n
-            for half in range(2):
-                h, l = split(turned(i, half, p))
-                rows = pl.ds(pl.multiple_of(i * TILE + half * BLK, BLK), BLK)
-                high[rows, lanes(p)] = h
-                low[rows, lanes(p)] = l
-        return carry
-
-    lax.fori_loop(0, STEPS, step, 0)
+        @pl.when(t < STEPS)
+        def _():
+            p = t // 2
+            for n in range(4):
+                i = (t % 2) * 4 + n
+                for half in range(2):
+                    h, l = split(turned(i, half, p))
+                    rows = pl.ds(pl.multiple_of(i * TILE + half * BLK, BLK), BLK)
+                    high[rows, lanes(p)] = h
+                    low[rows, lanes(p)] = l
+
+        return carry
+
+    lax.fori_loop(0, LEAD + CHUNKS + 3 * LAG, step, 0)
 
     def spread_drain(chunk, carry):
         for tree in range(3):
@@ -309,6 +320,79 @@
         ref = buf.at[here, rows_of(owner, offset, size)]
         put(ref, ref, side_s, ag_r.at[owner, part_index], va=va).wait_recv()
 
+    up, down = (vb + 1) % 8, (vb + 7) % 8
+    distances = ((vb - va + 8) % 8, (va - vb + 8) % 8)
+    owners = (va, side, *(m * 2 + yy for m in (right, left, across) for yy in (y, 1 - y)))
+
+    def chunk_rows(step, way):
+        owner = owners[7]
+        for n in range(7):
+            owner = jnp.where(step == n, owners[n], owner)
+        return rows_of(owner, way * HALF, HALF)
+
+    def ring(group, step, way, sems, **device):
+        ref = buf.at[group, chunk_rows(step, way)]
+        return put(ref, ref, sems[0].at[way, step], sems[1].at[way, step], **device)
+
+    pair_sems, far_sems, last_sems = (pair_s, pair_r), (far_s, far_r), (last_s, last_r)
+    lags = [(RING_LAG * d) // 2 for d in distances]
+    source = va == vb
+
+    def ring_step(t, carry):
+        for way in range(2):
+            step = t - lags[way]
+            toward = (up, down)[way]
+
+            @pl.when((step >= 0) & (step < 8 + EARLY))
+            def _():
+                late = step >= 8
+                local = jnp.where(late, step - 8, step)
+                ref = buf.at[jnp.where(late, far, aux), chunk_rows(local, way)]
+                along = put(ref, ref, ring_s.at[way, step], ring_r.at[way, step], vb=toward)
+
+                @pl.when(jnp.logical_not(source))
+                def _():
+                    along.wait_recv()
+
+                @pl.when(source & late)
+                def _():
+                    ring(far, local, way, far_sems, va=va).wait_recv()
+
+                if way == 0:
+
+                    @pl.when(source & (step == 1))
+                    def _():
+                        arrived(side, 0, SLICE, 0)
+
+                    for n, yy in enumerate((y, 1 - y)):
+
+                        @pl.when(source & (step == 6 + n))
+                        def _():
+                            arrived(across * 2 + yy, 0, HALF, 0)
+                            arrived(across * 2 + yy, HALF, HALF, 1)
+
+                @pl.when(distances[way] < 7)
+                def _():
+                    along.start()
+
+                @pl.when(jnp.logical_not(late))
+                def _():
+                    @pl.when(source | (step >= EARLY))
+                    def _():
+                        ring(aux, local, way, far_sems, aux=far).start()
+
+                    ring(aux, local, way, pair_sems, aux=partner).start()
+
+                @pl.when(late)
+                def _():
+                    ring(far, local, way, last_sems, aux=partner).start()
+
+        return carry
+
+    @pl.when(source)
+    def _():
+        ring_step(0, 0)
+
     for n, yy in enumerate((y, 1 - y)):
         from_left, from_right = left * 2 + yy, right * 2 + yy
         arrived(from_left, 0, SLICE, 0)
@@ -317,49 +401,14 @@
         arrived(from_right, 0, SLICE, 0)
         rows = rows_of(from_right, HALF, HALF)
         go(put(buf.at[here, rows], buf.at[home(left * 2 + y), rows], fwd_s.at[1, n], ag_r.at[from_right, 1], va=left * 2 + y))
-    arrived(side, 0, SLICE, 0)
-    for yy in range(2):
-        arrived(across * 2 + yy, 0, HALF, 0)
-        arrived(across * 2 + yy, HALF, HALF, 1)
-
-    up, down = (vb + 1) % 8, (vb + 7) % 8
-    distances = ((vb - va + 8) % 8, (va - vb + 8) % 8)
-    owners = (va, side, *(m * 2 + yy for m in (right, left, across) for yy in (y, 1 - y)))
-
-    def chunk_rows(step, way):
-        owner = owners[7]
-        for n in range(7):
-            owner = jnp.where(step == n, owners[n], owner)
-        return rows_of(owner, way * HALF, HALF)
-
-    def ring(group, step, way, sems, **device):
-        ref = buf.at[group, chunk_rows(step, way)]
-        return put(ref, ref, sems[0].at[way, step], sems[1].at[way, step], **device)
-
-    ring_sems, pair_sems, far_sems, last_sems = (ring_s, ring_r), (pair_s, pair_r), (far_s, far_r), (last_s, last_r)
-    lags = [(RING_LAG * d) // 2 for d in distances]
-
-    def ring_step(t, carry):
-        for way in range(2):
-            step = t - lags[way]
-            toward = (up, down)[way]
-
-            @pl.when((step >= 0) & (step < 8))
-            def _():
-                @pl.when(va != vb)
-                def _():
-                    ring(aux, step, way, ring_sems, va=va).wait_recv()
-
-                @pl.when(distances[way] < 7)
-                def _():
-                    ring(aux, step, way, ring_sems, vb=toward).start()
-
-                ring(aux, step, way, far_sems, aux=far).start()
-                ring(aux, step, way, pair_sems, aux=partner).start()
-
-        return carry
-
-    lax.fori_loop(0, 8 + (RING_LAG * 7) // 2, ring_step, 0)
+    lax.fori_loop(1, 8 + EARLY + (RING_LAG * 7) // 2, ring_step, 0)
+
+    @pl.when(jnp.logical_not(source))
+    def _():
+        arrived(side, 0, SLICE, 0)
+        for yy in (y, 1 - y):
+            arrived(across * 2 + yy, 0, HALF, 0)
+            arrived(across * 2 + yy, HALF, HALF, 1)
 
     def second_cols(n, carry):
         col_unpack(n, lambda rows, there: cols[rows, there] + 2.0 * buf[here, rows, there])
@@ -385,9 +434,10 @@
             rh, rl = row_high[...], row_low[...]
             ch, cl = col_high[...], col_low[...]
             result = dot_nt(rh, ch) + dot_nt(rh, cl) + dot_nt(rl, ch)
-            result = -result / ((column_a - occ[orbital]) + row_b) * SCALE
-            out[orbital, :, 0, :] = result[:, :TILE]
-            out[orbital, :, 1, :] = result[:, TILE:]
+            result = -result / ((column_a - occ[orbital]) + row_b)
+            for n in range(4):
+                place = pl.ds(orbital * (4 * TILE) + n % 2 * 2 + n // 2, TILE, stride=4)
+                out[place, :] = result[:, n * BLK : (n + 1) * BLK]
 
     def wait_chunks(group, sems):
         def one(step, carry):
@@ -401,10 +451,6 @@
         group = jnp.where(n == 0, aux, jnp.where(n == 1, partner, jnp.where(n == 2, far, corner)))
 
         @pl.when(n == 1)
-        def _():
-            wait_chunks(partner, pair_sems)
-
-        @pl.when(n == 2)
         def _():
             def onward(step, carry):
                 for way in range(2):
@@ -412,7 +458,8 @@
                     ring(far, step, way, last_sems, aux=partner).start()
                 return carry
 
-            lax.fori_loop(0, 8, onward, 0)
+            lax.fori_loop(EARLY, 8, onward, 0)
+            wait_chunks(partner, pair_sems)
 
         @pl.when(n == 3)
         def _():
@@ -425,17 +472,24 @@
 
     def ring_drain(step, carry):
         for way in range(2):
-            ring(aux, step, way, pair_sems, aux=partner).wait_send()
-            ring(aux, step, way, far_sems, aux=far).wait_send()
-            ring(far, step, way, last_sems, aux=partner).wait_send()
+
+            @pl.when(step < 8)
+            def _():
+                ring(aux, step, way, pair_sems, aux=partner).wait_send()
+                ring(far, step, way, last_sems, aux=partner).wait_send()
+
+                @pl.when(source | (step >= EARLY))
+                def _():
+                    ring(aux, step, way, far_sems, aux=far).wait_send()
 
             @pl.when(distances[way] < 7)
             def _():
-                ring(aux, step, way, ring_sems, vb=up).wait_send()
-
-        return carry
-
-    lax.fori_loop(0, 8, ring_drain, 0)
+                ref = buf.at[aux, chunk_rows(0, way)]
+                put(ref, ref, ring_s.at[way, step], ring_r.at[way, step], vb=up).wait_send()
+
+        return carry
+
+    lax.fori_loop(0, 8 + EARLY, ring_drain, 0)
     lax.fori_loop(0, CHUNKS, spread_drain, 0)
     for copy in sends:
         copy.wait_send()
@@ -445,9 +499,9 @@
     smem = pl.BlockSpec(memory_space=pltpu.SMEM)
     vmem = pl.BlockSpec(memory_space=pltpu.VMEM)
     dma = pltpu.SemaphoreType.DMA
-    return pl.pallas_call(
+    out = pl.pallas_call(
         kernel,
-        out_shape=jax.ShapeDtypeStruct((O, TILE, 2, TILE), F32),
+        out_shape=jax.ShapeDtypeStruct((ROWS * 4, BLK), F32),
         in_specs=[smem, smem, vmem, pl.BlockSpec(memory_space=pl.ANY)],
         out_specs=vmem,
         scratch_shapes=[
@@ -470,11 +524,12 @@
             dma((NPB, 2)), dma((3, CHUNKS, 2)), dma((3, CHUNKS)),
             dma((2, 2)), dma((2, 2)), dma, dma, dma((2, 2)), dma((4,)), dma((2, 2)), dma((4,)),
             dma((5,)), dma((8, 2)), dma((2, 2)),
-            dma((2, 8)), dma((2, 8)), dma((2, 8)), dma((2, 8)), dma((2, 8)), dma((2, 8)), dma((2, 8)), dma((2, 8)),
+            dma((2, 8 + EARLY)), dma((2, 8 + EARLY)), dma((2, 8)), dma((2, 8)), dma((2, 8)), dma((2, 8)), dma((2, 8)), dma((2, 8)),
         ],
         compiler_params=pltpu.CompilerParams(collective_id=0, has_side_effects=True, vmem_limit_bytes=VMEM_LIMIT),
         name="amplitudes",
-    )(domains, occ_energy, vir_energy.reshape(NVB, BLK), factors.reshape(NAUX * O, TILE))
+    )(domains.transpose(0, 2, 1), occ_energy, vir_energy.reshape(NVB, BLK), factors.reshape(NAUX * O, TILE))
+    return (out * SCALE).reshape(O, TILE, 2, 2, BLK).transpose(0, 1, 3, 2, 4).reshape(O, TILE, 2, TILE)
 
 
 def solution(mesh):

time: 143 us -> 144 us (level)
  local copies, waits for them, and re-layouts: 7.11 us -> 0 us
  other arithmetic: 0 us -> 4.47 us
  Pallas kernels: 135 us -> 139 us
    unnamed x2 -> x0, local copies, waits for them, and re-layouts: 7.11 us -> none
    mul x0 -> x1, other arithmetic: none -> 4.47 us  [body(): out * SCALE]
    pallas_call x1, Pallas kernels: 135 us -> 139 us  [body(): pl.pallas_call(kernel, out_shape=jax.ShapeDtypeStruct((ROWS * 4, BLK), F3...]
where the time goes in v3:
time: 144 us
  Pallas kernels  139 us (97%)
  other arithmetic  4.47 us (3%)
    pallas_call x1, Pallas kernels, body(): pl.pallas_call(kernel, out_shape=jax.ShapeDtypeStruct((ROWS * 4, BLK), F3...  139 us
    mul x1, other arithmetic, body(): out * SCALE  4.47 us

profile of v3, /device:TPU:14, one launch (start us, length us, event | category | flops | bytes accessed | tf_op | source)
XLA Modules:
  0.0 143.5 jit_solution(16594569293687489966)
XLA Ops:
  0.0 139.1 %amplitudes.1 = f32[8192,128]{1,0:T(8,128)} custom-call(s32[8,8,16]{2,1,0:T(8,128)} %bitcast.9, f32[8]{0:T(128)} %occ.1, f32[16,128]{1,0:T(8,128)} %bitcast.10, f32[8192,256]{1,0:T(8,128)} %bitcast.8), custom_call_target="tpu_custom_call" | custom-call | tf_op jit(solution)/shard_map/amplitudes/pallas_call | solution.py:502
  139.1 4.5 %broadcast_multiply_fusion = f32[8192,128]{1,0:T(8,128)} fusion(f32[8192,128]{1,0:T(8,128)} %amplitudes.1), kind=kLoop, calls=%fused_computation | loop fusion | flops 1048576 | bytes 8388608 | tf_op jit(solution)/shard_map/mul | solution.py:532

commit v4 on v3

--- a/solution.py
+++ b/solution.py
@@ -23,7 +23,9 @@
 CHUNKS = 8
 STEPS = 16
 LEAD = 5
-EARLY = 3
+QUARTER = SLICE // 4
+RING = 16
+EARLY = 2
 LAG = 2
 RING_LAG = 4
 SCALE = 8.0 * O * V / math.sqrt(NAUX)
@@ -311,14 +313,25 @@
     here = home(va)
     buf[here, mine] = part[mine] + ((recv[0] + recv[1]) + (recv[2] + recv[3])) + recv[4]
 
-    own = buf.at[here, mine]
-    targets = (right * 2 + y, left * 2 + y, x * 2 + 1 - y, right * 2 + 1 - y, left * 2 + 1 - y)
-    for n, target in enumerate(targets):
-        go(put(own, buf.at[home(target), mine], ag_s.at[n], ag_r.at[va, 0], va=target))
-
-    def arrived(owner, offset, size, part_index):
-        ref = buf.at[here, rows_of(owner, offset, size)]
-        put(ref, ref, side_s, ag_r.at[owner, part_index], va=va).wait_recv()
+    def gather(n, target, half):
+        rows = rows_of(va, half * HALF, HALF)
+        go(put(buf.at[here, rows], buf.at[home(target), rows], ag_s.at[n], ag_r.at[va, half], va=target))
+
+    sides = [m * 2 + yy for yy in (y, 1 - y) for m in (right, left)]
+    for n, target in enumerate(sides):
+        gather(n, target, n % 2)
+    for half in range(2):
+        gather(4 + half, side, half)
+    for n, target in enumerate(sides):
+        gather(6 + n, target, 1 - n % 2)
+
+    def arrived(owner, half):
+        ref = buf.at[here, rows_of(owner, half * HALF, HALF)]
+        put(ref, ref, side_s, ag_r.at[owner, half], va=va).wait_recv()
+
+    def arrived_rest(n):
+        for half in {1: (0, 1), 2: (0,), 3: (0,), 4: (1,), 5: (1,), 6: (0, 1), 7: (0, 1)}[n]:
+            arrived(owners[n], half)
 
     up, down = (vb + 1) % 8, (vb + 7) % 8
     distances = ((vb - va + 8) % 8, (va - vb + 8) % 8)
@@ -327,8 +340,8 @@
     def chunk_rows(step, way):
         owner = owners[7]
         for n in range(7):
-            owner = jnp.where(step == n, owners[n], owner)
-        return rows_of(owner, way * HALF, HALF)
+            owner = jnp.where(step // 2 == n, owners[n], owner)
+        return pl.ds(pl.multiple_of(owner * SLICE + way * HALF + step % 2 * QUARTER, QUARTER), QUARTER)
 
     def ring(group, step, way, sems, **device):
         ref = buf.at[group, chunk_rows(step, way)]
@@ -343,10 +356,10 @@
             step = t - lags[way]
             toward = (up, down)[way]
 
-            @pl.when((step >= 0) & (step < 8 + EARLY))
+            @pl.when((step >= 0) & (step < RING + EARLY))
             def _():
-                late = step >= 8
-                local = jnp.where(late, step - 8, step)
+                late = step >= RING
+                local = jnp.where(late, step - RING, step)
                 ref = buf.at[jnp.where(late, far, aux), chunk_rows(local, way)]
                 along = put(ref, ref, ring_s.at[way, step], ring_r.at[way, step], vb=toward)
 
@@ -359,17 +372,11 @@
                     ring(far, local, way, far_sems, va=va).wait_recv()
 
                 if way == 0:
-
-                    @pl.when(source & (step == 1))
-                    def _():
-                        arrived(side, 0, SLICE, 0)
-
-                    for n, yy in enumerate((y, 1 - y)):
-
-                        @pl.when(source & (step == 6 + n))
+                    for n in range(1, 8):
+
+                        @pl.when(source & (step == 2 * n))
                         def _():
-                            arrived(across * 2 + yy, 0, HALF, 0)
-                            arrived(across * 2 + yy, HALF, HALF, 1)
+                            arrived_rest(n)
 
                 @pl.when(distances[way] < 7)
                 def _():
@@ -392,23 +399,23 @@
     @pl.when(source)
     def _():
         ring_step(0, 0)
+        ring_step(1, 0)
 
     for n, yy in enumerate((y, 1 - y)):
         from_left, from_right = left * 2 + yy, right * 2 + yy
-        arrived(from_left, 0, SLICE, 0)
+        arrived(from_left, 0)
         rows = rows_of(from_left, 0, HALF)
         go(put(buf.at[here, rows], buf.at[home(right * 2 + y), rows], fwd_s.at[0, n], ag_r.at[from_left, 0], va=right * 2 + y))
-        arrived(from_right, 0, SLICE, 0)
+        arrived(from_right, 1)
         rows = rows_of(from_right, HALF, HALF)
         go(put(buf.at[here, rows], buf.at[home(left * 2 + y), rows], fwd_s.at[1, n], ag_r.at[from_right, 1], va=left * 2 + y))
-    lax.fori_loop(1, 8 + EARLY + (RING_LAG * 7) // 2, ring_step, 0)
+
+    lax.fori_loop(2, RING + EARLY + (RING_LAG * 7) // 2, ring_step, 0)
 
     @pl.when(jnp.logical_not(source))
     def _():
-        arrived(side, 0, SLICE, 0)
-        for yy in (y, 1 - y):
-            arrived(across * 2 + yy, 0, HALF, 0)
-            arrived(across * 2 + yy, HALF, HALF, 1)
+        for n in range(1, 8):
+            arrived_rest(n)
 
     def second_cols(n, carry):
         col_unpack(n, lambda rows, there: cols[rows, there] + 2.0 * buf[here, rows, there])
@@ -445,7 +452,7 @@
                 ring(group, step, way, sems, va=va).wait_recv()
             return carry
 
-        lax.fori_loop(0, 8, one, 0)
+        lax.fori_loop(0, RING, one, 0)
 
     def phase(n, carry):
         group = jnp.where(n == 0, aux, jnp.where(n == 1, partner, jnp.where(n == 2, far, corner)))
@@ -458,7 +465,7 @@
                     ring(far, step, way, last_sems, aux=partner).start()
                 return carry
 
-            lax.fori_loop(EARLY, 8, onward, 0)
+            lax.fori_loop(EARLY, RING, onward, 0)
             wait_chunks(partner, pair_sems)
 
         @pl.when(n == 3)
@@ -473,7 +480,7 @@
     def ring_drain(step, carry):
         for way in range(2):
 
-            @pl.when(step < 8)
+            @pl.when(step < RING)
             def _():
                 ring(aux, step, way, pair_sems, aux=partner).wait_send()
                 ring(far, step, way, last_sems, aux=partner).wait_send()
@@ -489,7 +496,7 @@
 
         return carry
 
-    lax.fori_loop(0, 8 + EARLY, ring_drain, 0)
+    lax.fori_loop(0, RING + EARLY, ring_drain, 0)
     lax.fori_loop(0, CHUNKS, spread_drain, 0)
     for copy in sends:
         copy.wait_send()
@@ -523,8 +530,8 @@
             pltpu.SMEM((4 * NPB * 3,), F32),
             dma((NPB, 2)), dma((3, CHUNKS, 2)), dma((3, CHUNKS)),
             dma((2, 2)), dma((2, 2)), dma, dma, dma((2, 2)), dma((4,)), dma((2, 2)), dma((4,)),
-            dma((5,)), dma((8, 2)), dma((2, 2)),
-            dma((2, 8 + EARLY)), dma((2, 8 + EARLY)), dma((2, 8)), dma((2, 8)), dma((2, 8)), dma((2, 8)), dma((2, 8)), dma((2, 8)),
+            dma((10,)), dma((8, 2)), dma((2, 2)),
+            dma((2, RING + EARLY)), dma((2, RING + EARLY)), dma((2, RING)), dma((2, RING)), dma((2, RING)), dma((2, RING)), dma((2, RING)), dma((2, RING)),
         ],
         compiler_params=pltpu.CompilerParams(collective_id=0, has_side_effects=True, vmem_limit_bytes=VMEM_LIMIT),
         name="amplitudes",

time: 144 us -> 146 us (1.014)
  Pallas kernels: 139 us -> 142 us
    pallas_call x1, Pallas kernels: 139 us -> 142 us  [body(): pl.pallas_call(kernel, out_shape=jax.ShapeDtypeStruct((ROWS * 4, BLK), F3...]
where the time goes in v4:
time: 146 us
  Pallas kernels  142 us (97%)
  other arithmetic  4.47 us (3%)
    pallas_call x1, Pallas kernels, body(): pl.pallas_call(kernel, out_shape=jax.ShapeDtypeStruct((ROWS * 4, BLK), F3...  142 us
    mul x1, other arithmetic, body(): out * SCALE  4.47 us

profile of v4, /device:TPU:14, one launch (start us, length us, event | category | flops | bytes accessed | tf_op | source)
XLA Modules:
  0.0 146.2 jit_solution(16396678397903671065)
XLA Ops:
  0.0 141.7 %amplitudes.1 = f32[8192,128]{1,0:T(8,128)} custom-call(s32[8,8,16]{2,1,0:T(8,128)} %bitcast.9, f32[8]{0:T(128)} %occ.1, f32[16,128]{1,0:T(8,128)} %bitcast.10, f32[8192,256]{1,0:T(8,128)} %bitcast.8), custom_call_target="tpu_custom_call" | custom-call | tf_op jit(solution)/shard_map/amplitudes/pallas_call | solution.py:509
  141.7 4.5 %broadcast_multiply_fusion = f32[8192,128]{1,0:T(8,128)} fusion(f32[8192,128]{1,0:T(8,128)} %amplitudes.1), kind=kLoop, calls=%fused_computation | loop fusion | flops 1048576 | bytes 8388608 | tf_op jit(solution)/shard_map/mul | solution.py:539

commit v5 on v4

--- a/solution.py
+++ b/solution.py
@@ -23,9 +23,9 @@
 CHUNKS = 8
 STEPS = 16
 LEAD = 5
-QUARTER = SLICE // 4
-RING = 16
-EARLY = 2
+RING = 8
+EARLY = 1
+ORDER = (4, 3, 5, 2, 6, 1, 7)
 LAG = 2
 RING_LAG = 4
 SCALE = 8.0 * O * V / math.sqrt(NAUX)
@@ -56,11 +56,10 @@
 
 def kernel(
     domains, occ, vir, factors, out,
-    raw, high, low, cols, col_high, col_low, total, part, buf, relay, merged, recv, row_high, row_low,
+    raw, high, low, cols, col_high, col_low, total, part, buf, recv, row_high, row_low,
     row_weights, col_weights,
     load, spread_s, spread_r,
-    relay_s, relay_r, side_s, side_r, near_s, near_r, merge_s, merge_r,
-    ag_s, ag_r, fwd_s, ring_s, ring_r, pair_s, pair_r, far_s, far_r, last_s, last_r,
+    rs_s, rs_r, ag_s, ag_r, ring_s, ring_r, pair_s, pair_r, far_s, far_r, last_s, last_r,
 ):
     va, vb, aux = lax.axis_index("va"), lax.axis_index("vb"), lax.axis_index("aux")
     x, y = va // 2, va % 2
@@ -174,7 +173,7 @@
 
         lax.fori_loop(0, CHUNKS, launch, 0)
 
-    def step(t, carry):
+    def relay(t):
         for tree in range(3):
             chunk = t - skews[tree]
 
@@ -188,20 +187,19 @@
                     def _():
                         spread(tree, chunk, k, member).start()
 
-        @pl.when(t < STEPS)
-        def _():
-            p = t // 2
-            for n in range(4):
-                i = (t % 2) * 4 + n
-                for half in range(2):
-                    h, l = split(turned(i, half, p))
-                    rows = pl.ds(pl.multiple_of(i * TILE + half * BLK, BLK), BLK)
-                    high[rows, lanes(p)] = h
-                    low[rows, lanes(p)] = l
-
-        return carry
-
-    lax.fori_loop(0, LEAD + CHUNKS + 3 * LAG, step, 0)
+    def prepare(t, carry):
+        relay(t)
+        p = t // 2
+        for n in range(4):
+            i = (t % 2) * 4 + n
+            for half in range(2):
+                h, l = split(turned(i, half, p))
+                rows = pl.ds(pl.multiple_of(i * TILE + half * BLK, BLK), BLK)
+                high[rows, lanes(p)] = h
+                low[rows, lanes(p)] = l
+        return carry
+
+    lax.fori_loop(0, STEPS, prepare, 0)
 
     def spread_drain(chunk, carry):
         for tree in range(3):
@@ -238,27 +236,31 @@
         col_unpack(n, lambda rows, there: cols[rows, there])
         return carry
 
-    lax.fori_loop(0, 4, first_cols, 0)
-    total[...] = jnp.zeros_like(total)
-
-    def dress(g, carry):
-        ch, cl = col_high[...], col_low[...]
-        parts_h, parts_l = [], []
-        for i in range(2):
-            rows = pl.ds(pl.multiple_of(g * PAIR + i * TILE, TILE), TILE)
+    def dress(j):
+        mine = slice(j * TILE, (j + 1) * TILE)
+
+        def one(g, carry):
+            if j == 0:
+                relay(STEPS + g)
+            ch, cl = col_high[mine, :], col_low[mine, :]
+            parts_h, parts_l = [], []
+            for i in range(2):
+                rows = pl.ds(pl.multiple_of(g * PAIR + i * TILE, TILE), TILE)
+                bh, bl = high[rows, :], low[rows, :]
+                direct = dot_nt(ch, bh) + dot_nt(ch, bl) + dot_nt(cl, bh)
+                energy = column_b[mine, :] + (row_a - occ[g * 2 + i])
+                h, l = split(-direct / energy)
+                parts_h.append(h)
+                parts_l.append(l)
+            th, tl = jnp.concatenate(parts_h, axis=1), jnp.concatenate(parts_l, axis=1)
+            rows = pl.ds(pl.multiple_of(g * PAIR, PAIR), PAIR)
             bh, bl = high[rows, :], low[rows, :]
-            direct = dot_nt(ch, bh) + dot_nt(ch, bl) + dot_nt(cl, bh)
-            energy = column_b + (row_a - occ[g * 2 + i])
-            h, l = split(-direct / energy)
-            parts_h.append(h)
-            parts_l.append(l)
-        th, tl = jnp.concatenate(parts_h, axis=1), jnp.concatenate(parts_l, axis=1)
-        rows = pl.ds(pl.multiple_of(g * PAIR, PAIR), PAIR)
-        bh, bl = high[rows, :], low[rows, :]
-        total[...] += dot_nn(th, bh) + dot_nn(th, bl) + dot_nn(tl, bh)
-        return carry
-
-    lax.fori_loop(0, 4, dress, 0)
+            total[mine, :] += dot_nn(th, bh) + dot_nn(th, bl) + dot_nn(tl, bh)
+            return carry
+
+        lax.fori_loop(2 * j, 2 * j + 2, first_cols, 0)
+        total[mine, :] = jnp.zeros((TILE, NAUX), F32)
+        lax.fori_loop(0, 4, one, 0)
 
     def pack(n, carry):
         rows = pl.ds(pl.multiple_of(n * BLK, BLK), BLK)
@@ -266,82 +268,60 @@
             part[rows, k * BLK : (k + 1) * BLK] = slot_of(n, k, lambda p: total[rows, p * BLK : (p + 1) * BLK])
         return carry
 
-    lax.fori_loop(0, 4, pack, 0)
-
-    def rows_of(owner, offset, size):
-        return pl.ds(pl.multiple_of(owner * SLICE + offset, HALF), size)
-
     def put(src, dst, s, r, **device):
         return pltpu.make_async_remote_copy(src, dst, s, r, device_id=device, device_id_type=MESH)
 
-    sends = []
-
-    def go(copy):
-        copy.start()
-        sends.append(copy)
-
-    for yy in range(2):
-        opposite = across * 2 + yy
-        go(put(part.at[rows_of(opposite, 0, HALF)], relay.at[0, yy], relay_s.at[0, yy], relay_r.at[0, yy], va=right * 2 + y))
-        go(put(part.at[rows_of(opposite, HALF, HALF)], relay.at[1, yy], relay_s.at[1, yy], relay_r.at[1, yy], va=left * 2 + y))
-    side = x * 2 + 1 - y
-    go(put(part.at[rows_of(side, 0, SLICE)], recv.at[4], side_s, side_r, va=side))
-    for yy in range(2):
-        slot = (yy + y) % 2
-        to_right, to_left = right * 2 + yy, left * 2 + yy
-        go(put(part.at[rows_of(to_right, HALF, HALF)], recv.at[slot, pl.ds(HALF, HALF)], near_s.at[0, yy], near_r.at[slot], va=to_right))
-        go(put(part.at[rows_of(to_left, 0, HALF)], recv.at[2 + slot, pl.ds(0, HALF)], near_s.at[1, yy], near_r.at[2 + slot], va=to_left))
-    for yy in range(2):
-        slot = (yy + y) % 2
-        to_right, to_left = right * 2 + yy, left * 2 + yy
-        put(relay.at[0, yy], relay.at[0, yy], relay_s.at[0, yy], relay_r.at[0, yy], va=va).wait_recv()
-        merged[0, yy] = part[rows_of(to_right, 0, HALF)] + relay[0, yy]
-        go(put(merged.at[0, yy], recv.at[slot, pl.ds(0, HALF)], merge_s.at[0, yy], merge_r.at[slot], va=to_right))
-        put(relay.at[1, yy], relay.at[1, yy], relay_s.at[1, yy], relay_r.at[1, yy], va=va).wait_recv()
-        merged[1, yy] = part[rows_of(to_left, HALF, HALF)] + relay[1, yy]
-        go(put(merged.at[1, yy], recv.at[2 + slot, pl.ds(HALF, HALF)], merge_s.at[1, yy], merge_r.at[2 + slot], va=to_left))
-    for slot in range(4):
-        put(merged.at[0, 0], recv.at[slot, pl.ds(0, HALF)], near_s.at[0, 0], near_r.at[slot], va=va).wait_recv()
-        put(merged.at[0, 0], recv.at[slot, pl.ds(0, HALF)], near_s.at[0, 0], merge_r.at[slot], va=va).wait_recv()
-    put(recv.at[4], recv.at[4], side_s, side_r, va=va).wait_recv()
-
-    mine = rows_of(va, 0, SLICE)
+    def piece(j, owner):
+        return pl.ds(pl.multiple_of(j * TILE + owner * HALF, HALF), HALF)
 
     def home(member):
         return jnp.where(member == vb, aux, 4)
 
     here = home(va)
-    buf[here, mine] = part[mine] + ((recv[0] + recv[1]) + (recv[2] + recv[3])) + recv[4]
-
-    def gather(n, target, half):
-        rows = rows_of(va, half * HALF, HALF)
-        go(put(buf.at[here, rows], buf.at[home(target), rows], ag_s.at[n], ag_r.at[va, half], va=target))
-
-    sides = [m * 2 + yy for yy in (y, 1 - y) for m in (right, left)]
-    for n, target in enumerate(sides):
-        gather(n, target, n % 2)
-    for half in range(2):
-        gather(4 + half, side, half)
-    for n, target in enumerate(sides):
-        gather(6 + n, target, 1 - n % 2)
-
-    def arrived(owner, half):
-        ref = buf.at[here, rows_of(owner, half * HALF, HALF)]
-        put(ref, ref, side_s, ag_r.at[owner, half], va=va).wait_recv()
-
-    def arrived_rest(n):
-        for half in {1: (0, 1), 2: (0,), 3: (0,), 4: (1,), 5: (1,), 6: (0, 1), 7: (0, 1)}[n]:
-            arrived(owners[n], half)
+    sends = []
+
+    def scatter(j):
+        lax.fori_loop(2 * j, 2 * j + 2, pack, 0)
+        for k in ORDER:
+            target = (va + k) % 8
+            copy = put(part.at[piece(j, target)], recv.at[j, k - 1], rs_s.at[j, k - 1], rs_r.at[j, k - 1], va=target)
+            copy.start()
+            sends.append(copy)
+
+    def gather(j):
+        for k in range(7):
+            put(recv.at[j, k], recv.at[j, k], rs_s.at[j, k], rs_r.at[j, k], va=va).wait_recv()
+        rows = piece(j, va)
+        value = ((recv[j, 0] + recv[j, 1]) + (recv[j, 2] + recv[j, 3])) + ((recv[j, 4] + recv[j, 5]) + recv[j, 6])
+        buf[here, rows] = part[rows] + value
+        for k in ORDER:
+            target = (va + k) % 8
+            copy = put(buf.at[here, rows], buf.at[home(target), rows], ag_s.at[j, k - 1], ag_r.at[j, va], va=target)
+            copy.start()
+            sends.append(copy)
+
+    def gathered(j, owner):
+        ref = buf.at[here, piece(j, owner)]
+        put(ref, ref, ag_s.at[j, 0], ag_r.at[j, owner], va=va).wait_recv()
+
+    dress(0)
+    scatter(0)
+    dress(1)
+    scatter(1)
+    gather(0)
 
     up, down = (vb + 1) % 8, (vb + 7) % 8
     distances = ((vb - va + 8) % 8, (va - vb + 8) % 8)
-    owners = (va, side, *(m * 2 + yy for m in (right, left, across) for yy in (y, 1 - y)))
+    owners = (va, x * 2 + 1 - y, *(m * 2 + yy for yy in (y, 1 - y) for m in (right, left)), across * 2 + y, across * 2 + 1 - y)
+
+    def owner_of(step, way):
+        owner = owners[6 + way]
+        for n in range(3):
+            owner = jnp.where(step % 4 == n, owners[2 * n + way], owner)
+        return owner
 
     def chunk_rows(step, way):
-        owner = owners[7]
-        for n in range(7):
-            owner = jnp.where(step // 2 == n, owners[n], owner)
-        return pl.ds(pl.multiple_of(owner * SLICE + way * HALF + step % 2 * QUARTER, QUARTER), QUARTER)
+        return piece(step // 4, owner_of(step, way))
 
     def ring(group, step, way, sems, **device):
         ref = buf.at[group, chunk_rows(step, way)]
@@ -371,12 +351,9 @@
                 def _():
                     ring(far, local, way, far_sems, va=va).wait_recv()
 
-                if way == 0:
-                    for n in range(1, 8):
-
-                        @pl.when(source & (step == 2 * n))
-                        def _():
-                            arrived_rest(n)
+                @pl.when(source & jnp.logical_not(late) & ((step % 4 != 0) | (way != 0)))
+                def _():
+                    gathered(local // 4, owner_of(local, way))
 
                 @pl.when(distances[way] < 7)
                 def _():
@@ -399,23 +376,15 @@
     @pl.when(source)
     def _():
         ring_step(0, 0)
-        ring_step(1, 0)
-
-    for n, yy in enumerate((y, 1 - y)):
-        from_left, from_right = left * 2 + yy, right * 2 + yy
-        arrived(from_left, 0)
-        rows = rows_of(from_left, 0, HALF)
-        go(put(buf.at[here, rows], buf.at[home(right * 2 + y), rows], fwd_s.at[0, n], ag_r.at[from_left, 0], va=right * 2 + y))
-        arrived(from_right, 1)
-        rows = rows_of(from_right, HALF, HALF)
-        go(put(buf.at[here, rows], buf.at[home(left * 2 + y), rows], fwd_s.at[1, n], ag_r.at[from_right, 1], va=left * 2 + y))
-
-    lax.fori_loop(2, RING + EARLY + (RING_LAG * 7) // 2, ring_step, 0)
+
+    gather(1)
+    lax.fori_loop(1, RING + EARLY + (RING_LAG * 7) // 2, ring_step, 0)
 
     @pl.when(jnp.logical_not(source))
     def _():
-        for n in range(1, 8):
-            arrived_rest(n)
+        for j in range(2):
+            for owner in owners[1:]:
+                gathered(j, owner)
 
     def second_cols(n, carry):
         col_unpack(n, lambda rows, there: cols[rows, there] + 2.0 * buf[here, rows, there])
@@ -509,7 +478,7 @@
     out = pl.pallas_call(
         kernel,
         out_shape=jax.ShapeDtypeStruct((ROWS * 4, BLK), F32),
-        in_specs=[smem, smem, vmem, pl.BlockSpec(memory_space=pl.ANY)],
+        in_specs=[smem, smem, vmem, pl.BlockSpec(memory_space=pltpu.HBM)],
         out_specs=vmem,
         scratch_shapes=[
             pltpu.VMEM((2, NAUX * O, BLK), F32),
@@ -521,16 +490,13 @@
             pltpu.VMEM((PAIR, NAUX), F32),
             pltpu.VMEM((PAIR, PACK), F32),
             pltpu.VMEM((5, PAIR, PACK), F32),
-            pltpu.VMEM((2, 2, HALF, PACK), F32),
-            pltpu.VMEM((2, 2, HALF, PACK), F32),
-            pltpu.VMEM((5, SLICE, PACK), F32),
+            pltpu.VMEM((2, 7, HALF, PACK), F32),
             pltpu.VMEM((TILE, NAUX), BF16),
             pltpu.VMEM((TILE, NAUX), BF16),
             pltpu.SMEM((O * 2 * NPB * 3,), F32),
             pltpu.SMEM((4 * NPB * 3,), F32),
             dma((NPB, 2)), dma((3, CHUNKS, 2)), dma((3, CHUNKS)),
-            dma((2, 2)), dma((2, 2)), dma, dma, dma((2, 2)), dma((4,)), dma((2, 2)), dma((4,)),
-            dma((10,)), dma((8, 2)), dma((2, 2)),
+            dma((2, 7)), dma((2, 7)), dma((2, 7)), dma((2, 8)),
             dma((2, RING + EARLY)), dma((2, RING + EARLY)), dma((2, RING)), dma((2, RING)), dma((2, RING)), dma((2, RING)), dma((2, RING)), dma((2, RING)),
         ],
         compiler_params=pltpu.CompilerParams(collective_id=0, has_side_effects=True, vmem_limit_bytes=VMEM_LIMIT),

time: 146 us -> 136 us (0.932)
  Pallas kernels: 142 us -> 131 us
    pallas_call x1, Pallas kernels: 142 us -> 131 us  [body(): pl.pallas_call(kernel, out_shape=jax.ShapeDtypeStruct((ROWS * 4, BLK), F3...]
where the time goes in v5:
time: 136 us; the launch traced here: 135 us
  Pallas kernels  131 us (96%)
  other arithmetic  4.47 us (3%)
    pallas_call x1, Pallas kernels, body(): pl.pallas_call(kernel, out_shape=jax.ShapeDtypeStruct((ROWS * 4, BLK), F3...  131 us
    mul x1, other arithmetic, body(): out * SCALE  4.47 us

profile of v5, /device:TPU:14, one launch (start us, length us, event | category | flops | bytes accessed | tf_op | source)
XLA Modules:
  0.0 135.4 jit_solution(6459631889557696825)
XLA Ops:
  0.0 130.9 %amplitudes.1 = f32[8192,128]{1,0:T(8,128)} custom-call(s32[8,8,16]{2,1,0:T(8,128)} %bitcast.9, f32[8]{0:T(128)} %occ.1, f32[16,128]{1,0:T(8,128)} %bitcast.10, f32[8192,256]{1,0:T(8,128)} %bitcast.8), custom_call_target="tpu_custom_call" | custom-call | tf_op jit(solution)/shard_map/amplitudes/pallas_call | solution.py:478
  130.9 4.5 %broadcast_multiply_fusion = f32[8192,128]{1,0:T(8,128)} fusion(f32[8192,128]{1,0:T(8,128)} %amplitudes.1), kind=kLoop, calls=%fused_computation | loop fusion | flops 1048576 | bytes 8388608 | tf_op jit(solution)/shard_map/mul | solution.py:505

commit v6 on v5

--- a/solution.py
+++ b/solution.py
@@ -278,6 +278,7 @@
         return jnp.where(member == vb, aux, 4)
 
     here = home(va)
+    source = va == vb
     sends = []
 
     def scatter(j):
@@ -294,11 +295,32 @@
         rows = piece(j, va)
         value = ((recv[j, 0] + recv[j, 1]) + (recv[j, 2] + recv[j, 3])) + ((recv[j, 4] + recv[j, 5]) + recv[j, 6])
         buf[here, rows] = part[rows] + value
-        for k in ORDER:
-            target = (va + k) % 8
-            copy = put(buf.at[here, rows], buf.at[home(target), rows], ag_s.at[j, k - 1], ag_r.at[j, va], va=target)
-            copy.start()
-            sends.append(copy)
+
+        @pl.when(jnp.logical_not(source))
+        def _():
+            deliver(j, va, vb, 0).start()
+
+    def deliver(j, owner, target, n):
+        rows = piece(j, owner)
+        return put(buf.at[here, rows], buf.at[home(target), rows], ag_s.at[j, n], ag_r.at[j, owner], va=target)
+
+    side = x * 2 + 1 - y
+    row_mates = [m * 2 + y for m in (across, right, left)]
+
+    def deliveries(act):
+        for j in range(2):
+            for n, target in enumerate((side, *row_mates)):
+
+                @pl.when(target != vb)
+                def _():
+                    act(j, va, target, 1 + n)
+
+    def passed_on(j, act):
+        for n, target in enumerate(row_mates):
+
+            @pl.when(target != vb)
+            def _():
+                act(j, side, target, 5 + n)
 
     def gathered(j, owner):
         ref = buf.at[here, piece(j, owner)]
@@ -329,8 +351,6 @@
 
     pair_sems, far_sems, last_sems = (pair_s, pair_r), (far_s, far_r), (last_s, last_r)
     lags = [(RING_LAG * d) // 2 for d in distances]
-    source = va == vb
-
     def ring_step(t, carry):
         for way in range(2):
             step = t - lags[way]
@@ -351,7 +371,7 @@
                 def _():
                     ring(far, local, way, far_sems, va=va).wait_recv()
 
-                @pl.when(source & jnp.logical_not(late) & ((step % 4 != 0) | (way != 0)))
+                @pl.when(source & jnp.logical_not(late) & ((step % 4 != 0) | ((way == 1) & (step == 0))))
                 def _():
                     gathered(local // 4, owner_of(local, way))
 
@@ -378,12 +398,33 @@
         ring_step(0, 0)
 
     gather(1)
-    lax.fori_loop(1, RING + EARLY + (RING_LAG * 7) // 2, ring_step, 0)
+    deliveries(lambda *which: deliver(*which).start())
+
+    @pl.when(source)
+    def _():
+        lax.fori_loop(1, 4, ring_step, 0)
+
+    @pl.when(jnp.logical_not(source))
+    def _():
+        gathered(0, side)
+
+    passed_on(0, lambda *which: deliver(*which).start())
+    gathered(1, side)
+    passed_on(1, lambda *which: deliver(*which).start())
+
+    def later_step(t, carry):
+        @pl.when(jnp.logical_not(source) | (t >= 4))
+        def _():
+            ring_step(t, 0)
+
+        return carry
+
+    lax.fori_loop(1, RING + EARLY + (RING_LAG * 7) // 2, later_step, 0)
 
     @pl.when(jnp.logical_not(source))
     def _():
         for j in range(2):
-            for owner in owners[1:]:
+            for owner in owners[2:]:
                 gathered(j, owner)
 
     def second_cols(n, carry):
@@ -469,6 +510,14 @@
     lax.fori_loop(0, CHUNKS, spread_drain, 0)
     for copy in sends:
         copy.wait_send()
+    for j in range(2):
+
+        @pl.when(jnp.logical_not(source))
+        def _():
+            deliver(j, va, vb, 0).wait_send()
+
+        passed_on(j, lambda *which: deliver(*which).wait_send())
+    deliveries(lambda *which: deliver(*which).wait_send())
 
 
 def body(factors, domains, occ_energy, vir_energy):
@@ -496,7 +545,7 @@
             pltpu.SMEM((O * 2 * NPB * 3,), F32),
             pltpu.SMEM((4 * NPB * 3,), F32),
             dma((NPB, 2)), dma((3, CHUNKS, 2)), dma((3, CHUNKS)),
-            dma((2, 7)), dma((2, 7)), dma((2, 7)), dma((2, 8)),
+            dma((2, 7)), dma((2, 7)), dma((2, 8)), dma((2, 8)),
             dma((2, RING + EARLY)), dma((2, RING + EARLY)), dma((2, RING)), dma((2, RING)), dma((2, RING)), dma((2, RING)), dma((2, RING)), dma((2, RING)),
         ],
         compiler_params=pltpu.CompilerParams(collective_id=0, has_side_effects=True, vmem_limit_bytes=VMEM_LIMIT),

time: 136 us -> 142 us (1.044); the launches traced: 135 us -> 140 us
  Pallas kernels: 131 us -> 135 us
    pallas_call x1, Pallas kernels: 131 us -> 135 us  [body(): pl.pallas_call(kernel, out_shape=jax.ShapeDtypeStruct((ROWS * 4, BLK), F3...]
where the time goes in v6:
time: 142 us; the launch traced here: 140 us
  Pallas kernels  135 us (95%)
  other arithmetic  4.47 us (3%)
    pallas_call x1, Pallas kernels, body(): pl.pallas_call(kernel, out_shape=jax.ShapeDtypeStruct((ROWS * 4, BLK), F3...  135 us
    mul x1, other arithmetic, body(): out * SCALE  4.47 us

profile of v6, /device:TPU:14, one launch (start us, length us, event | category | flops | bytes accessed | tf_op | source)
XLA Modules:
  0.0 139.7 jit_solution(10696540800168632332)
XLA Ops:
  0.0 135.3 %amplitudes.1 = f32[8192,128]{1,0:T(8,128)} custom-call(s32[8,8,16]{2,1,0:T(8,128)} %bitcast.9, f32[8]{0:T(128)} %occ.1, f32[16,128]{1,0:T(8,128)} %bitcast.10, f32[8192,256]{1,0:T(8,128)} %bitcast.8), custom_call_target="tpu_custom_call" | custom-call | tf_op jit(solution)/shard_map/amplitudes/pallas_call | solution.py:527
  135.3 4.5 %broadcast_multiply_fusion = f32[8192,128]{1,0:T(8,128)} fusion(f32[8192,128]{1,0:T(8,128)} %amplitudes.1), kind=kLoop, calls=%fused_computation | loop fusion | flops 1048576 | bytes 8388608 | tf_op jit(solution)/shard_map/mul | solution.py:554

commit v7 on v5

--- a/solution.py
+++ b/solution.py
@@ -32,7 +32,7 @@
 MESH = pl.DeviceIdType.MESH
 F32 = jnp.float32
 BF16 = jnp.bfloat16
-VMEM_LIMIT = 60 * 1024 * 1024
+VMEM_LIMIT = 48 * 1024 * 1024
 
 TREES = (
     {0: (1,), 1: (2, 5), 2: (3, 6), 5: (4,), 6: (7,)},
@@ -405,9 +405,11 @@
                         row_weights, orbital * 2 + half, p, lambda s: buf[group, here_rows, s * BLK : (s + 1) * BLK]
                     )
                     h, l = split(value + 2.0 * change)
-                    row_high[half * BLK : (half + 1) * BLK, block] = h
-                    row_low[half * BLK : (half + 1) * BLK, block] = l
-            rh, rl = row_high[...], row_low[...]
+                    row_high[i, half * BLK : (half + 1) * BLK, block] = h
+                    row_low[i, half * BLK : (half + 1) * BLK, block] = l
+        for i in range(2):
+            orbital = group * 2 + i
+            rh, rl = row_high[i], row_low[i]
             ch, cl = col_high[...], col_low[...]
             result = dot_nt(rh, ch) + dot_nt(rh, cl) + dot_nt(rl, ch)
             result = -result / ((column_a - occ[orbital]) + row_b)
@@ -475,6 +477,8 @@
     smem = pl.BlockSpec(memory_space=pltpu.SMEM)
     vmem = pl.BlockSpec(memory_space=pltpu.VMEM)
     dma = pltpu.SemaphoreType.DMA
+    inputs = (domains.transpose(0, 2, 1), occ_energy, vir_energy.reshape(NVB, BLK), factors.reshape(NAUX * O, TILE))
+    inputs = [pltpu.with_memory_space_constraint(array, pltpu.HBM) for array in inputs]
     out = pl.pallas_call(
         kernel,
         out_shape=jax.ShapeDtypeStruct((ROWS * 4, BLK), F32),
@@ -491,8 +495,8 @@
             pltpu.VMEM((PAIR, PACK), F32),
             pltpu.VMEM((5, PAIR, PACK), F32),
             pltpu.VMEM((2, 7, HALF, PACK), F32),
-            pltpu.VMEM((TILE, NAUX), BF16),
-            pltpu.VMEM((TILE, NAUX), BF16),
+            pltpu.VMEM((2, TILE, NAUX), BF16),
+            pltpu.VMEM((2, TILE, NAUX), BF16),
             pltpu.SMEM((O * 2 * NPB * 3,), F32),
             pltpu.SMEM((4 * NPB * 3,), F32),
             dma((NPB, 2)), dma((3, CHUNKS, 2)), dma((3, CHUNKS)),
@@ -501,7 +505,7 @@
         ],
         compiler_params=pltpu.CompilerParams(collective_id=0, has_side_effects=True, vmem_limit_bytes=VMEM_LIMIT),
         name="amplitudes",
-    )(domains.transpose(0, 2, 1), occ_energy, vir_energy.reshape(NVB, BLK), factors.reshape(NAUX * O, TILE))
+    )(*inputs)
     return (out * SCALE).reshape(O, TILE, 2, 2, BLK).transpose(0, 1, 3, 2, 4).reshape(O, TILE, 2, TILE)
 
 

time: 136 us -> 131 us (0.963)
  Pallas kernels: 131 us -> 128 us
  other arithmetic: 4.47 us -> 2.28 us
    pallas_call x1, Pallas kernels: 131 us -> 128 us  [body(): pl.pallas_call(kernel, out_shape=jax.ShapeDtypeStruct((ROWS * 4, BLK), F3...]
    mul x1, other arithmetic: 4.47 us -> 2.28 us  [body(): out * SCALE]
where the time goes in v7:
time: 131 us
  Pallas kernels  128 us (98%)
  other arithmetic  2.28 us (2%)
    pallas_call x1, Pallas kernels, body(): pl.pallas_call(kernel, out_shape=jax.ShapeDtypeStruct((ROWS * 4, BLK), F3...  128 us

profile of v7, /device:TPU:14, one launch (start us, length us, event | category | flops | bytes accessed | tf_op | source)
XLA Modules:
  0.0 130.7 jit_solution(3469802564609740800)
XLA Ops:
  0.0 128.4 %amplitudes.1 = f32[8192,128]{1,0:T(8,128)S(1)} custom-call(s32[8,8,16]{2,1,0:T(8,128)} %bitcast.9, f32[8]{0:T(128)} %occ.1, f32[16,128]{1,0:T(8,128)} %bitcast.10, f32[8192,256]{1,0:T(8,128)} %bitcast.8), custom_call_target="tpu_custom_call" | custom-call | tf_op jit(solution)/shard_map/amplitudes/pallas_call | solution.py:482
  128.4 2.3 %broadcast_multiply_fusion = f32[8192,128]{1,0:T(8,128)} fusion(f32[8192,128]{1,0:T(8,128)S(1)} %amplitudes.1), kind=kLoop, calls=%fused_computation | loop fusion | flops 1048576 | bytes 8388608 | tf_op jit(solution)/shard_map/mul | solution.py:509

commit v8 on v7

--- a/solution.py
+++ b/solution.py
@@ -24,7 +24,7 @@
 STEPS = 16
 LEAD = 5
 RING = 8
-EARLY = 1
+EARLY = 0
 ORDER = (4, 3, 5, 2, 6, 1, 7)
 LAG = 2
 RING_LAG = 4

time: 131 us -> 130 us (level)
  no operation moved by 1% of the time
where the time goes in v8:
time: 130 us
  Pallas kernels  127 us (98%)
  other arithmetic  2.28 us (2%)
    pallas_call x1, Pallas kernels, body(): pl.pallas_call(kernel, out_shape=jax.ShapeDtypeStruct((ROWS * 4, BLK), F3...  127 us

profile of v8, /device:TPU:14, one launch (start us, length us, event | category | flops | bytes accessed | tf_op | source)
XLA Modules:
  0.0 129.6 jit_solution(12632175976976497314)
XLA Ops:
  0.0 127.3 %amplitudes.1 = f32[8192,128]{1,0:T(8,128)S(1)} custom-call(s32[8,8,16]{2,1,0:T(8,128)} %bitcast.9, f32[8]{0:T(128)} %occ.1, f32[16,128]{1,0:T(8,128)} %bitcast.10, f32[8192,256]{1,0:T(8,128)} %bitcast.8), custom_call_target="tpu_custom_call" | custom-call | tf_op jit(solution)/shard_map/amplitudes/pallas_call | solution.py:482
  127.3 2.3 %broadcast_multiply_fusion = f32[8192,128]{1,0:T(8,128)} fusion(f32[8192,128]{1,0:T(8,128)S(1)} %amplitudes.1), kind=kLoop, calls=%fused_computation | loop fusion | flops 1048576 | bytes 8388608 | tf_op jit(solution)/shard_map/mul | solution.py:509
